TPU v7x, 32 devices: a whole 2x2x4 slice. The times are simulated.
32 devices in a mesh: gx: 16 (over z, x, core), gy: 2 (over y).
Axes of the slice: x: 2, y: 2, z: 4, core: 2. Of those that a mesh axis runs over, the one named last changes fastest.
Arguments:
- velocity: float32 [3, 14, 1536, 2048], P(None, None, 'gy', 'gx'), may hold values from -6 to 6
- operators: float32 [2, 768, 768], P(None, 'gx'), may hold values from -0.21875 to 0.21875
Outputs:
- tendency: float32 [3, 8, 1536, 2048], P(None, None, 'gy', 'gx')
All inputs are finite; a program needn't handle non-finite values.
Results may differ from a plain program's by a relative error of at most 0.000062.
Values sent between devices are 32-bit elements; how exact they have to be, the bound alone decides.
A program may use at most 192 MiB of HBM per device.

v0:
```python
import jax
import jax.numpy as jnp
from jax import lax
from jax.sharding import PartitionSpec as P


def extended(block, sides, width):
    for axis, dim in sides:
        count = lax.axis_size(axis)
        forward = [(i, i + 1) for i in range(count - 1)]
        forward.append((count - 1, 0))
        backward = [(target, source) for source, target in forward]
        low = lax.ppermute(
            lax.slice_in_dim(block, block.shape[dim] - width, None, axis=dim), axis, forward
        )
        high = lax.ppermute(lax.slice_in_dim(block, 0, width, axis=dim), axis, backward)
        block = jnp.concatenate([low, block, high], axis=dim)
    return block


def sixth_order(padded, along, length):

    def layer(offset):
        return lax.slice_in_dim(padded, 3 + offset, 3 + offset + length, axis=along)

    total = 45.0 * (layer(1) - layer(-1)) - 9.0 * (layer(2) - layer(-2)) + (layer(3) - layer(-3))
    return total / 60.0


def fold_lines(lines):
    halfway = lines.shape[2] // 2
    upper = lax.slice_in_dim(lines, 0, halfway, axis=2)
    lower = jnp.flip(lax.slice_in_dim(lines, halfway, 2 * halfway, axis=2), 2)
    return (upper + lower, upper - lower)


def shards(velocity, operators):
    width_x = velocity.shape[3]
    rows = velocity.shape[2]
    planes = velocity.shape[1] - 6
    inner = lax.slice_in_dim(velocity, 3, 3 + planes, axis=1)
    xflux = inner * inner[0]
    padded = extended(xflux, (("gx", 3),), 3)
    xdiv = sixth_order(padded, 3, width_x)
    zdiv = sixth_order(velocity * velocity[2], 1, planes)
    yflux = inner * inner[1]
    column_size = lax.axis_size("gy")
    position = lax.axis_index("gy")
    whole = lax.all_gather(yflux, "gy", axis=2, tiled=True)
    even, odd = fold_lines(whole)
    mirrored = position >= column_size // 2
    block = jnp.where(mirrored, column_size - 1 - position, position)
    first = block * rows
    own_columns = lax.dynamic_slice_in_dim(operators, first, rows, axis=2)
    piece = lax.all_gather(own_columns, "gx", axis=1, tiled=True)
    evenout = jnp.einsum("czkx,kj->czjx", even, piece[0], precision=lax.Precision.HIGHEST)
    oddout = jnp.einsum("czkx,kj->czjx", odd, piece[1], precision=lax.Precision.HIGHEST)
    ydiv = jnp.where(mirrored, jnp.flip(oddout - evenout, 2), evenout + oddout)
    return -(xdiv + ydiv + zdiv)


def solution(mesh):
    placed = (P(None, None, "gy", "gx"), P(None, "gx", None))
    return jax.shard_map(
        shards, mesh=mesh, in_specs=placed, out_specs=P(None, None, "gy", "gx"), check_vma=False
    )
```

profile of v0, /device:TPU:12, one launch (start us, length us, event | category | flops | bytes accessed | tf_op | source)
XLA Modules:
  0.0 569.1 jit_solution(7272350425149556710)
XLA Ops:
  6.5 0.0 all-gather.3.cloned.1.call-start
  6.5 17.3 %copy.3 = f32[3,14,768,128]{2,3,1,0:T(8,128)} copy(f32[3,14,768,128]{3,2,1,0:T(8,128)} %param.2) | data formatting | bytes 33030144 | tf_op args[0]
  23.8 6.1 %slice_bitcast_fusion.1 = (f32[8,768,128]{2,1,0:T(8,128)}, f32[8,768,128]{2,1,0:T(8,128)}) fusion(f32[3,14,768,128]{3,2,1,0:T(8,128)} %param.2), kind=kLoop, calls=%fused_computation.45 | loop fusion | bytes 12582912 | tf_op jit(solution)/shard_map/mul | solution.py:46
  29.9 2.4 copy.4
  32.3 3.5 copy.5
  35.8 10.4 %slice_multiply_fusion = (f32[3,8,768,128]{2,3,1,0:T(8,128)}, f32[3,8,768,128]{2,3,1,0:T(8,128)}) fusion(f32[3,14,768,128]{2,3,1,0:T(8,128)} %copy.3, f32[8,768,128]{1,2,0:T(8,128)} %copy.5, f32[8,768,128]{1,2,0:T(8,128)S(1)} %copy.4), kind=kLoop, calls=%fused_computation.41 | loop fusion | flops 4718592 | bytes 34603008 | tf_op jit(solution)/shard_map/mul | solution.py:46
  46.2 0.0 all-gather.3.cloned.1.call-update
  46.2 0.0 all-gather.5.cloned.1.call-start
  46.3 0.7 all-gather.5.cloned.1.call-update
  47.0 1.3 fusion.26
  48.3 0.9 collective-permute-start
  49.2 0.0 collective-permute-start.1
  49.2 5.9 %slice_bitcast_fusion = f32[14,768,128]{2,1,0:T(8,128)} fusion(f32[3,14,768,128]{3,2,1,0:T(8,128)} %param.2), kind=kLoop, calls=%fused_computation.44 | loop fusion | bytes 11010048 | tf_op jit(solution)/shard_map/mul | solution.py:45
  55.1 7.2 %copy.6 = f32[14,768,128]{1,2,0:T(8,128)} copy(f32[14,768,128]{2,1,0:T(8,128)} %slice_bitcast_fusion) | data formatting | bytes 11010048 | tf_op jit(solution)/shard_map/mul | solution.py:45
  62.3 16.7 %broadcast_multiply_fusion = f32[3,14,768,128]{2,3,1,0:T(8,128)} fusion(f32[3,14,768,128]{2,3,1,0:T(8,128)} %copy.3, f32[14,768,128]{1,2,0:T(8,128)} %copy.6), kind=kLoop, calls=%fused_computation.43 | loop fusion | flops 4128768 | bytes 38535168 | tf_op jit(solution)/shard_map/mul | solution.py:45
  79.0 192.0 %all-gather.3.cloned.1.call-done = f32[3,8,1536,128]{2,3,1,0:T(8,128)} async-done(((f32[3,8,768,128]{2,3,1,0:T(8,128)}), f32[3,8,1536,128]{2,3,1,0:T(8,128)}) %all-gather.3.cloned.1.call-update) | async-done | bytes 18874384 | tf_op jit(solution)/shard_map/all_gather | solution.py:49
  270.9 8.4 %slice.108 = f32[3,8,768,128]{2,3,1,0:T(8,128)} slice(f32[3,8,1536,128]{2,3,1,0:T(8,128)} %all-gather.3.cloned.1.call-done), slice={[0:3], [0:8], [768:1536], [0:128]} | slice | bytes 18874368 | tf_op jit(solution)/shard_map/slice | solution.py:33
  279.3 76.3 %rev.7 = f32[3,8,768,128]{2,3,1,0:T(8,128)} reverse(f32[3,8,768,128]{2,3,1,0:T(8,128)} %slice.108), dimensions={2} | reverse | bytes 18874368 | tf_op jit(solution)/shard_map/jit(_flip)/rev | solution.py:33
  355.6 0.0 all-gather.5.cloned.1.call-done
  355.6 0.0 copy-start
  355.6 0.0 copy-start.1
  355.6 28.2 %fusion.20 = f32[3,8,128,768]{3,2,1,0:T(8,128)} fusion(f32[3,8,768,128]{2,3,1,0:T(8,128)} %rev.7, f32[3,8,1536,128]{2,3,1,0:T(8,128)} %all-gather.3.cloned.1.call-done, f32[2,768,768]{2,1,0:T(8,128)} %all-gather.5.cloned.1.call-done), kind=kOutput, calls=%fused_computation.35 | convolution fusion | flops 21745631232 | bytes 30670848 | tf_op jit(solution)/shard_map/czkx,kj->czjx/dot_general | solution.py:56
  383.8 0.0 copy-done
  383.8 0.0 copy-done.1
  383.8 26.7 %fusion.22 = f32[3,8,128,768]{3,2,1,0:T(8,128)} fusion(f32[3,8,768,128]{2,3,1,0:T(8,128)S(1)} %copy-done, f32[3,8,1536,128]{2,3,1,0:T(8,128)S(1)} %copy-done.1, f32[2,768,768]{2,1,0:T(8,128)} %all-gather.5.cloned.1.call-done), kind=kOutput, calls=%fused_computation.37 | convolution fusion | flops 21745631232 | bytes 30670848 | tf_op jit(solution)/shard_map/czkx,kj->czjx/dot_general | solution.py:57
  410.5 11.6 %subtract_bitcast_fusion = f32[3,8,768,128]{2,3,1,0:T(8,128)} fusion(f32[3,8,128,768]{3,2,1,0:T(8,128)} %fusion.22, f32[3,8,128,768]{3,2,1,0:T(8,128)} %fusion.20), kind=kLoop, calls=%fused_computation.34 | loop fusion | flops 2359296 | bytes 28311552 | tf_op jit(solution)/shard_map/sub | solution.py:58
  422.1 76.2 %rev.8 = f32[3,8,768,128]{2,3,1,0:T(8,128)} reverse(f32[3,8,768,128]{2,3,1,0:T(8,128)} %subtract_bitcast_fusion), dimensions={2} | reverse | bytes 18874368 | tf_op jit(solution)/shard_map/jit(_flip)/rev | solution.py:58
  498.3 0.0 collective-permute-done
  498.3 0.0 collective-permute-done.1
  498.3 54.4 %fusion.8 = f32[3,8,768,128]{2,3,1,0:T(8,128)} fusion(f32[3,8,768,128]{2,3,1,0:T(8,128)} %get-tuple-element.6, f32[3,8,768,3]{2,3,1,0:T(4,128)S(1)} %collective-permute-done.1, f32[3,8,768,3]{2,3,1,0:T(4,128)S(1)} %collective-permute-done, f32[3,14,768,128]{2,3,1,0:T(8,128)} %broadcast_multiply_fusion, f32[3,8,768,128]{2,3,1,0:T(8,128)} %rev.8, ...), kind=kLoop, calls=%fused_computation.16 | loop fusion | flops 63700992 | bytes 104251392 | tf_op jit(solution)/shard_map/neg | solution.py:59
  552.7 9.6 %copy.8 = f32[3,8,768,128]{3,2,1,0:T(8,128)} copy(f32[3,8,768,128]{2,3,1,0:T(8,128)} %fusion.8) | data formatting | bytes 18874368 | tf_op jit(solution)/shard_map/neg | solution.py:59
Async XLA Ops:
  6.5 264.4 %all-gather.3.cloned.1.call-start = ((), (), s32[]{:S(2)}) async-start(), calls=%async_computation | async-start | bytes 28311552 | tf_op jit(solution)/shard_map/all_gather | solution.py:49
  46.2 309.4 %all-gather.5.cloned.1.call-start = ((), (), s32[]{:S(2)}) async-start(), calls=%async_computation.1 | async-start | bytes 5013504 | tf_op jit(solution)/shard_map/all_gather | solution.py:55
  48.3 450.0 %collective-permute-start = (f32[3,8,768,3]{2,3,1,0:T(4,128)S(1)}, f32[3,8,768,3]{2,3,1,0:T(4,128)S(1)}, u32[]{:S(2)}, u32[]{:S(2)}) collective-permute-start(f32[3,8,768,3]{2,3,1,0:T(4,128)S(1)} %get-tuple-element.9), channel_id=1, source_target_pairs={{2,0},{4,2},{6,4},{8,6},{10,8},{12,10},{14,12},{16,14},{18,16},{20... | collective-permute-start | bytes 663560 | tf_op jit(solution)/shard_map/ppermute | solution.py:16
  49.2 449.1 %collective-permute-start.1 = (f32[3,8,768,3]{2,3,1,0:T(4,128)S(1)}, f32[3,8,768,3]{2,3,1,0:T(4,128)S(1)}, u32[]{:S(2)}, u32[]{:S(2)}) collective-permute-start(f32[3,8,768,3]{2,3,1,0:T(4,128)S(1)} %get-tuple-element.10), channel_id=1, source_target_pairs={{0,2},{2,4},{4,6},{6,8},{8,10},{10,12},{12,14},{14,16},{16,18},{18... | collective-permute-start | bytes 663560 | tf_op jit(solution)/shard_map/ppermute | solution.py:13
  355.6 28.2 %copy-start = (f32[3,8,768,128]{2,3,1,0:T(8,128)S(1)}, f32[3,8,768,128]{2,3,1,0:T(8,128)}, u32[]{:S(2)}) copy-start(f32[3,8,768,128]{2,3,1,0:T(8,128)} %rev.7) | copy-start | bytes 28311556
  355.6 28.2 %copy-start.1 = (f32[3,8,1536,128]{2,3,1,0:T(8,128)S(1)}, f32[3,8,1536,128]{2,3,1,0:T(8,128)}, u32[]{:S(2)}) copy-start(f32[3,8,1536,128]{2,3,1,0:T(8,128)} %all-gather.3.cloned.1.call-done) | copy-start | bytes 56623108
Sparse Core Ops, SparseCore 0:
  46.4 224.5 all-gather.2
  273.2 54.4 all-gather.4
where the time goes:
time: 581 us; the launch traced here: 569 us
  local copies, waits for them, and re-layouts  214 us (37%)
  waiting for transfers between devices  193 us (33%)
  other arithmetic  93 us (16%)
  matrix products  54.9 us (9%)
  between operations  13.4 us (2%)
    all_gather x1, waiting for transfers between devices, shards(): whole = lax.all_gather(yflux, 'gy', axis=2, tiled=True)  192 us
    rev x1, local copies, waits for them, and re-layouts, fold_lines(): lower = jnp.flip(lax.slice_in_dim(lines, halfway, 2 * halfway, axis=2), 2)  76.3 us
    rev x1, local copies, waits for them, and re-layouts, shards(): ydiv = jnp.where(mirrored, jnp.flip(oddout - evenout, 2), evenout + oddout)  76.2 us
    neg x1, other arithmetic, shards(): return -(xdiv + ydiv + zdiv)  54.4 us
    dot_general x1, matrix products, shards(): jnp.einsum('czkx,kj->czjx', even, piece[0], precision=lax.Precision.HIGHEST)  28.2 us
    dot_general x1, matrix products, shards(): jnp.einsum('czkx,kj->czjx', odd, piece[1], precision=lax.Precision.HIGHEST)  26.7 us
    unnamed x5, local copies, waits for them, and re-layouts  17.3 us
    mul x1, other arithmetic, shards(): zdiv = sixth_order(velocity * velocity[2], 1, planes)  16.7 us
  transfers between devices with their start and end apart: 4, of which 1 were waited for; matrix products, arithmetic and copies ran while one was open for 45% of the time, Pallas kernels for 0%

commit v1 on v0

v1 whole, which is shorter than its diff:
```python
import functools

import jax
import jax.numpy as jnp
import numpy as np
from jax import lax
from jax.experimental import pallas as pl
from jax.experimental.pallas import tpu as pltpu
from jax.sharding import PartitionSpec as P

RIM = 3
WEIGHTS = ((1, 45.0), (2, -9.0), (3, 1.0))
CHUNKS = (2, 2, 2, 1, 1)


def stencil_matrices(width):
    inside = np.zeros((width, width), np.float32)
    rim = np.zeros((8, width), np.float32)
    for m in range(width):
        for step, weight in WEIGHTS:
            for offset, signed in ((step, weight), (-step, -weight)):
                at = m + offset
                if at < 0:
                    rim[at + RIM, m] = signed
                elif at >= width:
                    rim[at - width + RIM, m] = signed
                else:
                    inside[at, m] = signed
    return inside, rim


def split(value):
    high = value.astype(jnp.bfloat16)
    low = (value - high.astype(jnp.float32)).astype(jnp.bfloat16)
    return high, low


def dot(left, right, contract=((1,), (0,)), precision=None):
    return lax.dot_general(
        left, right, (contract, ((), ())),
        preferred_element_type=jnp.float32, precision=precision,
    )


def stencil_kernel(vel_ref, halo_ref, inside_ref, rim_ref, out_ref):
    planes = out_ref.shape[1]
    inside = inside_ref[...]
    rim = rim_ref[...]
    for z in range(planes):
        for i in range(3):
            high, low = split(vel_ref[i, RIM + z] * vel_ref[0, RIM + z])
            total = dot(high, inside) + dot(low, inside)
            edges = halo_ref[i, z] * halo_ref[0, z]
            total += dot(edges, rim, ((0,), (0,)), lax.Precision.HIGHEST)
            for step, weight in WEIGHTS:
                up, down = RIM + z + step, RIM + z - step
                total += weight * (
                    vel_ref[i, up] * vel_ref[2, up] - vel_ref[i, down] * vel_ref[2, down]
                )
            out_ref[i, z] = total * (-1.0 / 60.0)


def stencils(velocity, halo):
    _, held, rows, width = velocity.shape
    planes = held - 2 * RIM
    tile = 128 if rows % 128 == 0 else rows
    inside, rim = stencil_matrices(width)
    return pl.pallas_call(
        stencil_kernel,
        grid=(rows // tile,),
        in_specs=[
            pl.BlockSpec((3, held, tile, width), lambda t: (0, 0, t, 0)),
            pl.BlockSpec((3, planes, 8, tile), lambda t: (0, 0, 0, t)),
            pl.BlockSpec((width, width), lambda t: (0, 0)),
            pl.BlockSpec((8, width), lambda t: (0, 0)),
        ],
        out_specs=pl.BlockSpec((3, planes, tile, width), lambda t: (0, 0, t, 0)),
        out_shape=jax.ShapeDtypeStruct((3, planes, rows, width), jnp.float32),
        compiler_params=pltpu.CompilerParams(vmem_limit_bytes=24 << 20),
        cost_estimate=pl.CostEstimate(
            flops=12 * planes * rows * width * width,
            bytes_accessed=4 * 3 * (held + planes) * rows * width,
            transcendentals=0,
        ),
        name="stencils",
    )(velocity, halo, jnp.asarray(inside, jnp.bfloat16), jnp.asarray(rim))


def flip_or_same(size, flipped):
    row = lax.broadcasted_iota(jnp.int32, (size, size), 0)
    column = lax.broadcasted_iota(jnp.int32, (size, size), 1)
    wanted = jnp.where(flipped == 1, size - 1 - column, column)
    return jnp.where(row == wanted, 1.0, 0.0).astype(jnp.bfloat16)


def weights_kernel(flags, piece_ref, high_ref, low_ref):
    entry = pl.program_id(0) * 4
    block, same, flip_in, flip_out = (flags[entry + k] for k in range(4))
    depth, tile = high_ref.shape[2], high_ref.shape[1]
    at = pl.ds(pl.multiple_of(block * depth, 8), depth)
    even, odd = piece_ref[0, at, :], piece_ref[1, at, :]
    combined = even + jnp.where(same == 1, odd, -odd)
    combined = jnp.where(flip_out == 1, combined, -combined)
    turn_in = flip_or_same(depth, flip_in)
    turn_out = flip_or_same(tile, flip_out)
    for part, out_ref in zip(split(combined), (high_ref, low_ref)):
        turned = dot(part, turn_in, ((0,), (0,))).astype(jnp.bfloat16)
        out_ref[0] = dot(turn_out, turned).astype(jnp.bfloat16)


def column_weights(piece, position, count):
    _, halfway, rows = piece.shape
    tile = 256 if rows % 256 == 0 else rows
    tiles = rows // tile
    source = lax.rem(position + jnp.arange(count, dtype=jnp.int32), count)
    low_half = source >= count // 2
    mine = position >= count // 2
    flags = jnp.stack(
        [
            jnp.where(low_half, count - 1 - source, source),
            (low_half == mine).astype(jnp.int32),
            low_half.astype(jnp.int32),
            jnp.broadcast_to(mine, (count,)).astype(jnp.int32),
        ],
        axis=1,
    ).reshape(-1)
    shape = jax.ShapeDtypeStruct((count, rows, rows), jnp.bfloat16)
    out_spec = pl.BlockSpec((1, tile, rows), lambda s, g, flags: (s, g, 0))
    return pl.pallas_call(
        weights_kernel,
        grid_spec=pltpu.PrefetchScalarGridSpec(
            num_scalar_prefetch=1,
            grid=(count, tiles),
            in_specs=[
                pl.BlockSpec(
                    (2, halfway, tile),
                    lambda s, g, flags: (
                        0, 0, jnp.where(flags[s * 4 + 3] == 1, tiles - 1 - g, g)
                    ),
                )
            ],
            out_specs=[out_spec, out_spec],
        ),
        out_shape=[shape, shape],
        compiler_params=pltpu.CompilerParams(vmem_limit_bytes=24 << 20),
        cost_estimate=pl.CostEstimate(
            flops=8 * count * rows * rows * rows,
            bytes_accessed=count * rows * (8 * halfway + 4 * rows),
            transcendentals=0,
        ),
        name="weights",
    )(flags, piece)


def column_kernel(first, count, acc_ref, high_ref, low_ref, *refs):
    *lines, out_ref = refs
    total = None
    for s in range(count):
        line = lines[s]
        v = line[1, 0]
        high, low = split(jnp.concatenate([line[i, 0] * v for i in range(3)], axis=1))
        w_high, w_low = high_ref[first + s], low_ref[first + s]
        term = dot(w_high, high) + (dot(w_high, low) + dot(w_low, high))
        total = term if total is None else total + term
    width = out_ref.shape[3]
    for i in range(3):
        out_ref[i, 0] = acc_ref[i, 0] + total[:, i * width:(i + 1) * width]


def add_column(acc, weights, first, lines, offset, start, planes):
    high, low = weights
    _, _, rows, width = acc.shape
    count = len(lines)
    block = (3, 1, rows, width)
    held = pl.BlockSpec(block, lambda z: (0, start + z, 0, 0))
    whole = pl.BlockSpec(high.shape, lambda z: (0, 0, 0), pipeline_mode=pl.Buffered(1))
    if count == 1:
        whole = pl.BlockSpec(
            (1,) + high.shape[1:], lambda z: (first, 0, 0), pipeline_mode=pl.Buffered(1)
        )
        first_in_block = 0
    else:
        first_in_block = first
    return pl.pallas_call(
        functools.partial(column_kernel, first_in_block, count),
        grid=(planes,),
        in_specs=[held, whole, whole]
        + [pl.BlockSpec(block, lambda z: (0, offset + z, 0, 0))] * count,
        out_specs=held,
        out_shape=jax.ShapeDtypeStruct(acc.shape, acc.dtype),
        input_output_aliases={0: 0},
        compiler_params=pltpu.CompilerParams(vmem_limit_bytes=32 << 20),
        cost_estimate=pl.CostEstimate(
            flops=18 * planes * count * rows * rows * width,
            bytes_accessed=4 * 3 * planes * (2 + count) * rows * width + 4 * count * rows * rows,
            transcendentals=0,
        ),
        name="column",
    )(acc, high, low, *lines)


def around(count, step):
    return [((i + step) % count, i) for i in range(count)]


def shards(velocity, operators):
    _, held, rows, width = velocity.shape
    planes = held - 2 * RIM
    ring = lax.axis_size("gx")
    count = lax.axis_size("gy")
    position = lax.axis_index("gy")

    starts, sizes, at = [], [], 0
    for size in CHUNKS:
        size = min(size, planes - at)
        if size > 0:
            starts.append(at)
            sizes.append(size)
            at += size
    if at < planes:
        starts.append(at)
        sizes.append(planes - at)
    arrived = []
    for start, size in zip(starts, sizes):
        part = lax.slice_in_dim(velocity, RIM + start, RIM + start + size, axis=1)
        arrived.append([lax.ppermute(part, "gy", around(count, s)) for s in range(1, count)])

    inner = lax.slice_in_dim(velocity, RIM, RIM + planes, axis=1)
    left = jnp.swapaxes(lax.slice_in_dim(inner, width - RIM, width, axis=3), 2, 3)
    right = jnp.swapaxes(lax.slice_in_dim(inner, 0, RIM, axis=3), 2, 3)
    left = lax.ppermute(left, "gx", around(ring, ring - 1))
    right = lax.ppermute(right, "gx", around(ring, 1))
    nothing = jnp.zeros((3, planes, 8 - 2 * RIM, rows), jnp.float32)
    halo = jnp.concatenate([left, right, nothing], axis=2)

    block = jnp.where(position >= count // 2, count - 1 - position, position)
    own_columns = lax.dynamic_slice_in_dim(operators, block * rows, rows, axis=2)
    piece = lax.all_gather(own_columns, "gx", axis=1, tiled=True)
    weights = column_weights(piece, position, count)

    acc = stencils(velocity, halo)
    acc = add_column(acc, weights, 0, [velocity], RIM, 0, planes)
    for start, size, lines in zip(starts, sizes, arrived):
        acc = add_column(acc, weights, 1, lines, 0, start, size)
    return acc


def solution(mesh):
    placed = (P(None, None, "gy", "gx"), P(None, "gx", None))
    return jax.shard_map(
        shards, mesh=mesh, in_specs=placed, out_specs=P(None, None, "gy", "gx"), check_vma=False
    )
```

time: 581 us -> 258 us (0.44); the launches traced: 569 us -> 256 us
  local copies, waits for them, and re-layouts: 214 us -> 49.2 us
  other arithmetic: 93 us -> 1.29 us
  waiting for transfers between devices: 193 us -> 111 us
  Pallas kernels: 0 us -> 73.4 us
  matrix products: 54.9 us -> 0 us
  starting transfers between devices: 0.91 us -> 7.22 us
    all_gather x1 -> x0, waiting for transfers between devices: 192 us -> none  [shards(): whole = lax.all_gather(yflux, 'gy', axis=2, tiled=True)]
    rev x2 -> x0, local copies, waits for them, and re-layouts: 153 us -> none  [the longest x1 76.3 us: fold_lines(): lower = jnp.flip(lax.slice_in_dim(lines, halfway, 2 * halfway, axis=2), 2)]
    ppermute x2 -> x7, waiting for transfers between devices: 0.01 us -> 110 us  [the longest x5 110 us: shards(): lax.ppermute(part, 'gy', around(count, s))]
    pallas_call x0 -> x8, Pallas kernels: none -> 73.4 us  [the longest x6 48 us: add_column(): pl.pallas_call(functools.partial(column_kernel, first_in_block, count), g...]
    dot_general x2 -> x0, matrix products: 54.9 us -> none  [the longest x1 28.2 us: shards(): jnp.einsum('czkx,kj->czjx', even, piece[0], precision=lax.Precision.HIGHEST)]
    neg x1 -> x0, other arithmetic: 54.4 us -> none  [shards(): return -(xdiv + ydiv + zdiv)]
    mul x2 -> x0, other arithmetic: 27.1 us -> none  [the longest x1 16.7 us: shards(): zdiv = sixth_order(velocity * velocity[2], 1, planes)]
    mul x5 -> x0, local copies, waits for them, and re-layouts: 25.1 us -> none  [the longest x2 13.1 us: shards(): zdiv = sixth_order(velocity * velocity[2], 1, planes)]
  transfers between devices with their start and end apart: 4 -> 8, of which waited for: 1 -> 4; matrix products, arithmetic and copies ran while one was open for 45% -> 14% of each run, Pallas kernels for 0% -> 27%
where the time goes in v1:
time: 258 us; the launch traced here: 256 us
  waiting for transfers between devices  111 us (43%)
  Pallas kernels  73.4 us (28%)
  local copies, waits for them, and re-layouts  49.2 us (19%)
  between operations  13.5 us (5%)
  starting transfers between devices  7.22 us (3%)
    ppermute x5, waiting for transfers between devices, shards(): lax.ppermute(part, 'gy', around(count, s))  110 us
    pallas_call x6, Pallas kernels, add_column(): pl.pallas_call(functools.partial(column_kernel, first_in_block, count), g...  48 us
    unnamed x14, local copies, waits for them, and re-layouts  27.4 us
    pallas_call x1, Pallas kernels, stencils(): pl.pallas_call(stencil_kernel, grid=(rows // tile,), in_specs=[pl.BlockSp...  15.5 us
    slice x1, local copies, waits for them, and re-layouts, shards(): lax.slice_in_dim(inner, width - RIM, width, axis=3)  12.1 us
    pallas_call x1, Pallas kernels, column_weights(): pl.pallas_call(weights_kernel, grid_spec=pltpu.PrefetchScalarGridSpec(num...  9.89 us
    slice x2, local copies, waits for them, and re-layouts, shards(): part = lax.slice_in_dim(velocity, RIM + start, RIM + start + size, axis=1)  9.51 us
  transfers between devices with their start and end apart: 8, of which 4 were waited for; matrix products, arithmetic and copies ran while one was open for 14% of the time, Pallas kernels for 27%

profile of v1, /device:TPU:12, one launch (start us, length us, event | category | flops | bytes accessed | tf_op | source)
XLA Modules:
  0.0 255.7 jit_solution(5726673814634221426)
XLA Ops:
  6.5 0.0 all-gather.2.cloned.1.call-start
  6.5 0.7 all-gather.2.cloned.1.call-update
  7.3 12.1 %fusion.4 = (f32[3,8,768,3]{3,2,1,0:T(8,128)}, f32[3,8,768,3]{3,2,1,0:T(8,128)}) fusion(f32[3,14,768,128]{3,2,1,0:T(8,128)} %refs_0_.1), kind=kLoop, calls=%fused_computation.11 | loop fusion | bytes 884736 | tf_op jit(solution)/shard_map/slice | solution.py:229
  19.3 5.7 %copy.13 = f32[3,8,768,3]{2,3,1,0:T(4,128)S(1)} copy(f32[3,8,768,3]{3,2,1,0:T(8,128)} %get-tuple-element.14) | data formatting | bytes 442368
  25.0 0.1 collective-permute-start
  25.1 6.3 %copy.14 = f32[3,8,768,3]{2,3,1,0:T(4,128)} copy(f32[3,8,768,3]{3,2,1,0:T(8,128)} %get-tuple-element.15) | data formatting | bytes 442368
  31.4 2.6 %collective-permute-start.1 = (f32[3,8,3,768]{3,2,1,0:T(4,128)}, f32[3,8,3,768]{3,2,1,0:T(4,128)}, u32[]{:S(2)}, u32[]{:S(2)}) collective-permute-start(f32[3,8,3,768]{3,2,1,0:T(4,128)} %bitcast.1), channel_id=1, source_target_pairs={{2,0},{4,2},{6,4},{8,6},{10,8},{12,10},{14,12},{16,14},{18,16},{20... | collective-permute-start | bytes 663560 | tf_op jit(solution)/shard_map/ppermute | solution.py:232
  34.0 6.3 %fusion.3 = (f32[3,2,768,128]{3,2,1,0:T(8,128)}, f32[3,2,768,128]{3,2,1,0:T(8,128)}, f32[3,2,768,128]{3,2,1,0:T(8,128)}) fusion(f32[3,14,768,128]{3,2,1,0:T(8,128)} %refs_0_.1), kind=kLoop, calls=%fused_computation.10 | loop fusion | bytes 14155776 | tf_op jit(solution)/shard_map/slice | solution.py:225
  40.2 0.5 collective-permute-start.2
  40.8 1.5 collective-permute-start.3
  42.3 0.5 collective-permute-start.4
  42.8 0.1 pad.3.clone
  42.9 0.0 copy-start.3
  42.9 3.3 %fusion.2 = (f32[3,1,768,128]{3,2,1,0:T(8,128)}, f32[3,1,768,128]{3,2,1,0:T(8,128)}) fusion(f32[3,14,768,128]{3,2,1,0:T(8,128)} %refs_0_.1), kind=kLoop, calls=%fused_computation.9 | loop fusion | bytes 4718592 | tf_op jit(solution)/shard_map/slice | solution.py:225
  46.1 0.1 add_add_fusion
  46.2 0.1 reshape.48.flags
  46.3 0.1 pad.6.clone
  46.4 0.0 collective-permute-done
  46.4 0.0 copy-start.5
  46.4 0.7 copy-done.5
  47.1 1.5 collective-permute-start.5
  48.6 0.0 collective-permute-done.1
  48.6 0.6 collective-permute-start.6
  49.1 1.2 maximum_maximum_fusion.halo_ref
  50.3 0.0 copy-done.3
  50.3 0.0 copy-start
  50.4 5.9 %copy-done = f32[3,14,768,128]{3,2,1,0:T(8,128)S(1)} copy-done((f32[3,14,768,128]{3,2,1,0:T(8,128)S(1)}, f32[3,14,768,128]{3,2,1,0:T(8,128)}, u32[]{:S(2)}) %copy-start) | copy-done | bytes 16515096
  56.2 0.0 copy-start.2
  56.2 0.8 copy-done.2
  57.0 15.5 %stencils.1.acc_ref = f32[3,8,768,128]{3,2,1,0:T(8,128)} custom-call(f32[3,14,768,128]{3,2,1,0:T(8,128)S(1)} %copy-done, f32[3,8,8,768]{3,2,1,0:T(8,128)S(1)} %maximum_maximum_fusion.halo_ref, bf16[128,128]{1,0:T(8,128)(2,1)S(1)} %copy-done.2, f32[8,128]{1,0:T(8,128)S(1)} %copy-done.3), custom_call_target="tpu_custom_call" | custom-call | flops 1207959552 | bytes 25952256 | tf_op jit(solution)/shard_map/stencils/pallas_call | solution.py:68
  72.5 0.0 all-gather.2.cloned.1.call-done.piece_ref
  72.5 0.0 copy-start.4
  72.5 2.3 copy-done.4
  74.8 9.9 %weights.1 = (bf16[2,768,768]{2,1,0:T(8,128)(2,1)S(1)}, bf16[2,768,768]{2,1,0:T(8,128)(2,1)S(1)}) custom-call(s32[8]{0:T(128)S(1)} %reshape.48.flags, f32[2,768,768]{2,1,0:T(8,128)S(1)} %copy-done.4), custom_call_target="tpu_custom_call" | custom-call | flops 7247757312 | bytes 14155776 | tf_op jit(solution)/shard_map/weights/pallas_call | solution.py:129
  84.7 0.0 copy-start.1
  84.7 5.7 %copy-done.1 = f32[3,14,768,128]{3,2,1,0:T(8,128)S(1)} copy-done((f32[3,14,768,128]{3,2,1,0:T(8,128)S(1)}, f32[3,14,768,128]{3,2,1,0:T(8,128)}, u32[]{:S(2)}) %copy-start.1) | copy-done | bytes 16515096
  90.4 19.1 %column.6.acc_ref = f32[3,8,768,128]{3,2,1,0:T(8,128)} custom-call(f32[3,8,768,128]{3,2,1,0:T(8,128)} %stencils.1.acc_ref, bf16[2,768,768]{2,1,0:T(8,128)(2,1)S(1)} %get-tuple-element.7.high_ref, bf16[2,768,768]{2,1,0:T(8,128)(2,1)S(1)} %get-tuple-element.8.low_ref, f32[3,14,768,128]{3,2,1,0:T(8,128)S(1)} %copy-done.1), custom_call_target="tpu_custom_call", output_to_operand_aliasing={{}: (0, {})} | custom-call | flops 10871635968 | bytes 30670848 | tf_op jit(solution)/shard_map/column/pallas_call | solution.py:184
  109.6 0.0 collective-permute-done.2.refs_0_
  109.6 6.7 %column.7.acc_ref = f32[3,8,768,128]{3,2,1,0:T(8,128)} custom-call(f32[3,8,768,128]{3,2,1,0:T(8,128)} %column.6.acc_ref, bf16[2,768,768]{2,1,0:T(8,128)(2,1)S(1)} %get-tuple-element.7.high_ref, bf16[2,768,768]{2,1,0:T(8,128)(2,1)S(1)} %get-tuple-element.8.low_ref, f32[3,2,768,128]{3,2,1,0:T(8,128)} %collective-permute-done.2.refs_0_), custom_call_target="tpu_custom_call", output_to_operand_aliasing={{}: (0, {})} | custom-call | flops 2717908992 | bytes 9437184 | tf_op jit(solution)/shard_map/column/pallas_call | solution.py:184
  116.3 29.0 %collective-permute-done.3.refs_0_ = f32[3,2,768,128]{3,2,1,0:T(8,128)} collective-permute-done((f32[3,2,768,128]{3,2,1,0:T(8,128)}, f32[3,2,768,128]{3,2,1,0:T(8,128)}, u32[]{:S(2)}, u32[]{:S(2)}) %collective-permute-start.3) | collective-permute-done | bytes 2359328 | tf_op jit(solution)/shard_map/ppermute | solution.py:226
  145.3 6.7 %column.8.acc_ref = f32[3,8,768,128]{3,2,1,0:T(8,128)} custom-call(f32[3,8,768,128]{3,2,1,0:T(8,128)} %column.7.acc_ref, bf16[2,768,768]{2,1,0:T(8,128)(2,1)S(1)} %get-tuple-element.7.high_ref, bf16[2,768,768]{2,1,0:T(8,128)(2,1)S(1)} %get-tuple-element.8.low_ref, f32[3,2,768,128]{3,2,1,0:T(8,128)} %collective-permute-done.3.refs_0_), custom_call_target="tpu_custom_call", output_to_operand_aliasing={{}: (0, {})} | custom-call | flops 2717908992 | bytes 9437184 | tf_op jit(solution)/shard_map/column/pallas_call | solution.py:184
  152.0 43.7 %collective-permute-done.4.refs_0_ = f32[3,2,768,128]{3,2,1,0:T(8,128)S(1)} collective-permute-done((f32[3,2,768,128]{3,2,1,0:T(8,128)}, f32[3,2,768,128]{3,2,1,0:T(8,128)S(1)}, u32[]{:S(2)}, u32[]{:S(2)}) %collective-permute-start.4) | collective-permute-done | bytes 2359328 | tf_op jit(solution)/shard_map/ppermute | solution.py:226
  195.8 6.4 %column.9.acc_ref = f32[3,8,768,128]{3,2,1,0:T(8,128)} custom-call(f32[3,8,768,128]{3,2,1,0:T(8,128)} %column.8.acc_ref, bf16[2,768,768]{2,1,0:T(8,128)(2,1)S(1)} %get-tuple-element.7.high_ref, bf16[2,768,768]{2,1,0:T(8,128)(2,1)S(1)} %get-tuple-element.8.low_ref, f32[3,2,768,128]{3,2,1,0:T(8,128)S(1)} %collective-permute-done.4.refs_0_), custom_call_target="tpu_custom_call", output_to_operand_aliasing={{}: (0, {})} | custom-call | flops 2717908992 | bytes 9437184 | tf_op jit(solution)/shard_map/column/pallas_call | solution.py:184
  202.1 18.9 %collective-permute-done.5.refs_0_ = f32[3,1,768,128]{3,2,1,0:T(8,128)S(1)} collective-permute-done((f32[3,1,768,128]{3,2,1,0:T(8,128)}, f32[3,1,768,128]{3,2,1,0:T(8,128)S(1)}, u32[]{:S(2)}, u32[]{:S(2)}) %collective-permute-start.5) | collective-permute-done | bytes 1179680 | tf_op jit(solution)/shard_map/ppermute | solution.py:226
  221.0 4.3 %column.10.acc_ref = f32[3,8,768,128]{3,2,1,0:T(8,128)} custom-call(f32[3,8,768,128]{3,2,1,0:T(8,128)} %column.9.acc_ref, bf16[2,768,768]{2,1,0:T(8,128)(2,1)S(1)} %get-tuple-element.7.high_ref, bf16[2,768,768]{2,1,0:T(8,128)(2,1)S(1)} %get-tuple-element.8.low_ref, f32[3,1,768,128]{3,2,1,0:T(8,128)S(1)} %collective-permute-done.5.refs_0_), custom_call_target="tpu_custom_call", output_to_operand_aliasing={{}: (0, {})} | custom-call | flops 1358954496 | bytes 5898240 | tf_op jit(solution)/shard_map/column/pallas_call | solution.py:184
  225.3 18.9 %collective-permute-done.6.refs_0_ = f32[3,1,768,128]{3,2,1,0:T(8,128)} collective-permute-done((f32[3,1,768,128]{3,2,1,0:T(8,128)}, f32[3,1,768,128]{3,2,1,0:T(8,128)}, u32[]{:S(2)}, u32[]{:S(2)}) %collective-permute-start.6) | collective-permute-done | bytes 1179680 | tf_op jit(solution)/shard_map/ppermute | solution.py:226
  244.2 4.7 %column.11 = f32[3,8,768,128]{3,2,1,0:T(8,128)} custom-call(f32[3,8,768,128]{3,2,1,0:T(8,128)} %column.10.acc_ref, bf16[2,768,768]{2,1,0:T(8,128)(2,1)S(1)} %get-tuple-element.7.high_ref, bf16[2,768,768]{2,1,0:T(8,128)(2,1)S(1)} %get-tuple-element.8.low_ref, f32[3,1,768,128]{3,2,1,0:T(8,128)} %collective-permute-done.6.refs_0_), custom_call_target="tpu_custom_call", output_to_operand_aliasing={{}: (0, {})} | custom-call | flops 1358954496 | bytes 5898240 | tf_op jit(solution)/shard_map/column/pallas_call | solution.py:184
  (3 shorter events, 0.0 us)
Async XLA Ops:
  6.5 66.0 %all-gather.2.cloned.1.call-start = ((), (), s32[]{:S(2)}) async-start(), calls=%async_computation | async-start | bytes 5013504 | tf_op jit(solution)/shard_map/all_gather | solution.py:238
  25.0 21.4 %collective-permute-start = (f32[3,8,3,768]{3,2,1,0:T(4,128)S(1)}, f32[3,8,3,768]{3,2,1,0:T(4,128)S(1)}, u32[]{:S(2)}, u32[]{:S(2)}) collective-permute-start(f32[3,8,3,768]{3,2,1,0:T(4,128)S(1)} %bitcast.3), channel_id=1, source_target_pairs={{30,0},{0,2},{2,4},{4,6},{6,8},{8,10},{10,12},{12,14},{14,16},{16,... | collective-permute-start | bytes 663560 | tf_op jit(solution)/shard_map/ppermute | solution.py:231
  31.4 17.2 %collective-permute-start.1 = (f32[3,8,3,768]{3,2,1,0:T(4,128)}, f32[3,8,3,768]{3,2,1,0:T(4,128)}, u32[]{:S(2)}, u32[]{:S(2)}) collective-permute-start(f32[3,8,3,768]{3,2,1,0:T(4,128)} %bitcast.1), channel_id=1, source_target_pairs={{2,0},{4,2},{6,4},{8,6},{10,8},{12,10},{14,12},{16,14},{18,16},{20... | collective-permute-start | bytes 663560 | tf_op jit(solution)/shard_map/ppermute | solution.py:232
  40.2 69.3 %collective-permute-start.2 = (f32[3,2,768,128]{3,2,1,0:T(8,128)}, f32[3,2,768,128]{3,2,1,0:T(8,128)}, u32[]{:S(2)}, u32[]{:S(2)}) collective-permute-start(f32[3,2,768,128]{3,2,1,0:T(8,128)} %get-tuple-element.13), channel_id=1, source_target_pairs={{1,0},{0,1},{3,2},{2,3},{5,4},{4,5},{7,6},{6,7},{9,8},{8,9},{11,10... | collective-permute-start | bytes 7077896 | tf_op jit(solution)/shard_map/ppermute | solution.py:226
  40.8 104.5 %collective-permute-start.3 = (f32[3,2,768,128]{3,2,1,0:T(8,128)}, f32[3,2,768,128]{3,2,1,0:T(8,128)}, u32[]{:S(2)}, u32[]{:S(2)}) collective-permute-start(f32[3,2,768,128]{3,2,1,0:T(8,128)} %get-tuple-element.12), channel_id=1, source_target_pairs={{1,0},{0,1},{3,2},{2,3},{5,4},{4,5},{7,6},{6,7},{9,8},{8,9},{11,10... | collective-permute-start | bytes 7077896 | tf_op jit(solution)/shard_map/ppermute | solution.py:226
  42.3 153.5 %collective-permute-start.4 = (f32[3,2,768,128]{3,2,1,0:T(8,128)}, f32[3,2,768,128]{3,2,1,0:T(8,128)S(1)}, u32[]{:S(2)}, u32[]{:S(2)}) collective-permute-start(f32[3,2,768,128]{3,2,1,0:T(8,128)} %get-tuple-element.11), channel_id=1, source_target_pairs={{1,0},{0,1},{3,2},{2,3},{5,4},{4,5},{7,6},{6,7},{9,8},{8,9},{11,10... | collective-permute-start | bytes 7077896 | tf_op jit(solution)/shard_map/ppermute | solution.py:226
  42.9 7.5 %copy-start.3 = (f32[8,128]{1,0:T(8,128)S(1)}, f32[8,128]{1,0:T(8,128)}, u32[]{:S(2)}) copy-start(f32[8,128]{1,0:T(8,128)} %constant.20.clone.rim_ref) | copy-start | bytes 12292
  46.4 0.7 copy-start.5
  47.1 173.9 %collective-permute-start.5 = (f32[3,1,768,128]{3,2,1,0:T(8,128)}, f32[3,1,768,128]{3,2,1,0:T(8,128)S(1)}, u32[]{:S(2)}, u32[]{:S(2)}) collective-permute-start(f32[3,1,768,128]{3,2,1,0:T(8,128)} %get-tuple-element.10), channel_id=1, source_target_pairs={{1,0},{0,1},{3,2},{2,3},{5,4},{4,5},{7,6},{6,7},{9,8},{8,9},{11,10... | collective-permute-start | bytes 3538952 | tf_op jit(solution)/shard_map/ppermute | solution.py:226
  48.6 195.6 %collective-permute-start.6 = (f32[3,1,768,128]{3,2,1,0:T(8,128)}, f32[3,1,768,128]{3,2,1,0:T(8,128)}, u32[]{:S(2)}, u32[]{:S(2)}) collective-permute-start(f32[3,1,768,128]{3,2,1,0:T(8,128)} %get-tuple-element.9), channel_id=1, source_target_pairs={{1,0},{0,1},{3,2},{2,3},{5,4},{4,5},{7,6},{6,7},{9,8},{8,9},{11,10... | collective-permute-start | bytes 3538952 | tf_op jit(solution)/shard_map/ppermute | solution.py:226
  50.3 5.9 %copy-start = (f32[3,14,768,128]{3,2,1,0:T(8,128)S(1)}, f32[3,14,768,128]{3,2,1,0:T(8,128)}, u32[]{:S(2)}) copy-start(f32[3,14,768,128]{3,2,1,0:T(8,128)} %refs_0_.1) | copy-start | bytes 49545220
  56.2 0.8 copy-start.2
  72.5 2.3 copy-start.4
  84.7 5.7 %copy-start.1 = (f32[3,14,768,128]{3,2,1,0:T(8,128)S(1)}, f32[3,14,768,128]{3,2,1,0:T(8,128)}, u32[]{:S(2)}) copy-start(f32[3,14,768,128]{3,2,1,0:T(8,128)} %refs_0_.1) | copy-start | bytes 49545220
Sparse Core Ops, SparseCore 0:
  9.6 55.0 all-gather.1

commit v2 on v1

--- a/solution.py
+++ b/solution.py
@@ -10,7 +10,7 @@
 
 RIM = 3
 WEIGHTS = ((1, 45.0), (2, -9.0), (3, 1.0))
-CHUNKS = (2, 2, 2, 1, 1)
+CHUNKS = (1, 6, 1)
 
 
 def stencil_matrices(width):
@@ -97,8 +97,15 @@
     entry = pl.program_id(0) * 4
     block, same, flip_in, flip_out = (flags[entry + k] for k in range(4))
     depth, tile = high_ref.shape[2], high_ref.shape[1]
-    at = pl.ds(pl.multiple_of(block * depth, 8), depth)
-    even, odd = piece_ref[0, at, :], piece_ref[1, at, :]
+    strip = piece_ref.shape[3]
+    pairs = depth // (2 * strip)
+    even, odd = (
+        jnp.concatenate(
+            [piece_ref[core, block * pairs + r, c] for r in range(pairs) for core in range(2)],
+            axis=0,
+        )
+        for c in range(2)
+    )
     combined = even + jnp.where(same == 1, odd, -odd)
     combined = jnp.where(flip_out == 1, combined, -combined)
     turn_in = flip_or_same(depth, flip_in)
@@ -109,7 +116,8 @@
 
 
 def column_weights(piece, position, count):
-    _, halfway, rows = piece.shape
+    _, pairs, _, strip, rows = piece.shape
+    halfway = 2 * pairs * strip
     tile = 256 if rows % 256 == 0 else rows
     tiles = rows // tile
     source = lax.rem(position + jnp.arange(count, dtype=jnp.int32), count)
@@ -133,9 +141,9 @@
             grid=(count, tiles),
             in_specs=[
                 pl.BlockSpec(
-                    (2, halfway, tile),
+                    (2, pairs, 2, strip, tile),
                     lambda s, g, flags: (
-                        0, 0, jnp.where(flags[s * 4 + 3] == 1, tiles - 1 - g, g)
+                        0, 0, 0, 0, jnp.where(flags[s * 4 + 3] == 1, tiles - 1 - g, g)
                     ),
                 )
             ],
@@ -203,6 +211,25 @@
     return [((i + step) % count, i) for i in range(count)]
 
 
+def gather_rows(block, last):
+    ring = lax.axis_size("gx")
+    me = lax.axis_index("gx")
+    if ring & (ring - 1):
+        rows = lax.all_gather(block, "gx", axis=0)
+        return jnp.swapaxes(rows.reshape((ring // 2, 2) + block.shape), 0, 1), last
+
+    def exchange(held, bit, join):
+        other = lax.ppermute(held, "gx", [(i, i ^ (1 << bit)) for i in range(ring)])
+        upper = (me >> bit) & 1 == 1
+        return join([jnp.where(upper, other, held), jnp.where(upper, held, other)], 0)
+
+    held = block[None]
+    for bit in range(1, ring.bit_length() - 1):
+        held = exchange(held, bit, jnp.concatenate)
+    held, last = lax.optimization_barrier((held, last))
+    return exchange(held, 0, jnp.stack), last
+
+
 def shards(velocity, operators):
     _, held, rows, width = velocity.shape
     planes = held - 2 * RIM
@@ -210,20 +237,28 @@
     count = lax.axis_size("gy")
     position = lax.axis_index("gy")
 
-    starts, sizes, at = [], [], 0
+    cuts, at = [], 0
     for size in CHUNKS:
-        size = min(size, planes - at)
-        if size > 0:
-            starts.append(at)
-            sizes.append(size)
+        if at < planes:
+            cuts.append((at, min(size, planes - at)))
             at += size
     if at < planes:
-        starts.append(at)
-        sizes.append(planes - at)
-    arrived = []
-    for start, size in zip(starts, sizes):
-        part = lax.slice_in_dim(velocity, RIM + start, RIM + start + size, axis=1)
-        arrived.append([lax.ppermute(part, "gy", around(count, s)) for s in range(1, count)])
+        cuts.append((at, planes - at))
+
+    def plane_range(field, start, size):
+        return lax.slice_in_dim(field, RIM + start, RIM + start + size, axis=1)
+
+    def send(part):
+        return [lax.ppermute(part, "gy", around(count, s)) for s in range(1, count)]
+
+    velocity, part = lax.optimization_barrier((velocity, plane_range(velocity, *cuts[0])))
+    arrived = [send(part)]
+    velocity, part = lax.optimization_barrier((velocity, plane_range(velocity, *cuts[1])))
+    arrived.append(send(part))
+    for k, cut in enumerate(cuts[2:]):
+        arrived[k], part = lax.optimization_barrier((arrived[k], plane_range(velocity, *cut)))
+        arrived.append(send(part))
+    operators, arrived[0] = lax.optimization_barrier((operators, arrived[0]))
 
     inner = lax.slice_in_dim(velocity, RIM, RIM + planes, axis=1)
     left = jnp.swapaxes(lax.slice_in_dim(inner, width - RIM, width, axis=3), 2, 3)
@@ -235,12 +270,12 @@
 
     block = jnp.where(position >= count // 2, count - 1 - position, position)
     own_columns = lax.dynamic_slice_in_dim(operators, block * rows, rows, axis=2)
-    piece = lax.all_gather(own_columns, "gx", axis=1, tiled=True)
+    acc = stencils(velocity, halo)
+    piece, acc = gather_rows(own_columns, acc)
     weights = column_weights(piece, position, count)
 
-    acc = stencils(velocity, halo)
     acc = add_column(acc, weights, 0, [velocity], RIM, 0, planes)
-    for start, size, lines in zip(starts, sizes, arrived):
+    for (start, size), lines in zip(cuts, arrived):
         acc = add_column(acc, weights, 1, lines, 0, start, size)
     return acc
 

time: 258 us -> 223 us (0.86)
  waiting for transfers between devices: 111 us -> 94 us
  between operations: 13.5 us -> 0.15 us
  local copies, waits for them, and re-layouts: 49.2 us -> 40.6 us
  other arithmetic: 1.29 us -> 6.76 us
  Pallas kernels: 73.4 us -> 68.2 us
    ppermute x5 -> x7, waiting for transfers between devices: 110 us -> 65.7 us  [the longest x3 43.9 us: send(): return [lax.ppermute(part, 'gy', around(count, s)) for s in range(1, count)]]
    ppermute x1, waiting for transfers between devices: 0.01 us -> 21.8 us  [shards(): right = lax.ppermute(right, 'gx', around(ring, 1))]
    optimization_barrier x0 -> x1, local copies, waits for them, and re-layouts: none -> 17.3 us  [shards(): lax.optimization_barrier((velocity, plane_range(velocity, *cuts[1])))]
    unnamed x14 -> x10, local copies, waits for them, and re-layouts: 27.4 us -> 11.4 us
    slice x3, local copies, waits for them, and re-layouts: 21.6 us -> 10.3 us  [plane_range(): return lax.slice_in_dim(field, RIM + start, RIM + start + size, axis=1)]
    ppermute x1, waiting for transfers between devices: 0.01 us -> 6.54 us  [shards(): left = lax.ppermute(left, 'gx', around(ring, ring - 1))]
    pallas_call x6 -> x4, Pallas kernels: 48 us -> 42.8 us  [add_column(): pl.pallas_call(functools.partial(column_kernel, first_in_block, count), g...]
    ppermute x5 -> x7, starting transfers between devices: 4.57 us -> 7.09 us  [the longest x4 4.67 us: exchange(): other = lax.ppermute(held, 'gx', [(i, i ^ 1 << bit) for i in range(ring)])]
  transfers between devices with their start and end apart: 8 -> 9, of which waited for: 4 -> 8; matrix products, arithmetic and copies ran while one was open for 14% -> 16% of each run, Pallas kernels for 27% -> 29%
where the time goes in v2:
time: 223 us; the launch traced here: 219 us
  waiting for transfers between devices  94 us (42%)
  Pallas kernels  68.2 us (31%)
  local copies, waits for them, and re-layouts  40.6 us (18%)
  starting transfers between devices  9.78 us (4%)
  other arithmetic  6.76 us (3%)
    ppermute x3, waiting for transfers between devices, send(): return [lax.ppermute(part, 'gy', around(count, s)) for s in range(1, count)]  43.9 us
    pallas_call x4, Pallas kernels, add_column(): pl.pallas_call(functools.partial(column_kernel, first_in_block, count), g...  42.8 us
    ppermute x1, waiting for transfers between devices, shards(): right = lax.ppermute(right, 'gx', around(ring, 1))  21.8 us
    ppermute x4, waiting for transfers between devices, exchange(): other = lax.ppermute(held, 'gx', [(i, i ^ 1 << bit) for i in range(ring)])  21.7 us
    optimization_barrier x1, local copies, waits for them, and re-layouts, shards(): lax.optimization_barrier((velocity, plane_range(velocity, *cuts[1])))  17.3 us
    pallas_call x1, Pallas kernels, stencils(): pl.pallas_call(stencil_kernel, grid=(rows // tile,), in_specs=[pl.BlockSp...  15.5 us
    unnamed x10, local copies, waits for them, and re-layouts  11.4 us
    slice x3, local copies, waits for them, and re-layouts, plane_range(): return lax.slice_in_dim(field, RIM + start, RIM + start + size, axis=1)  10.3 us
  transfers between devices with their start and end apart: 9, of which 8 were waited for; matrix products, arithmetic and copies ran while one was open for 16% of the time, Pallas kernels for 29%

profile of v2, /device:TPU:12, one launch (start us, length us, event | category | flops | bytes accessed | tf_op | source)
XLA Modules:
  0.0 219.4 jit_solution(10359348470170170145)
XLA Ops:
  0.0 1.3 slice.18
  1.4 0.6 collective-permute-start
  1.9 6.5 %slice.19 = f32[3,6,768,128]{3,2,1,0:T(8,128)} slice(f32[3,14,768,128]{3,2,1,0:T(8,128)} %refs_0_), slice={[0:3], [4:10], [0:768], [0:128]} | slice | bytes 14155776 | tf_op jit(solution)/shard_map/slice | solution.py:249
  8.4 0.0 copy-start.4
  8.4 2.4 %slice.20 = f32[3,1,768,128]{3,2,1,0:T(8,128)} slice(f32[3,14,768,128]{3,2,1,0:T(8,128)} %refs_0_), slice={[0:3], [10:11], [0:768], [0:128]} | slice | bytes 2359296 | tf_op jit(solution)/shard_map/slice | solution.py:249
  10.9 18.3 %collective-permute-done.refs_0_ = f32[3,1,768,128]{3,2,1,0:T(8,128)S(1)} collective-permute-done((f32[3,1,768,128]{3,2,1,0:T(8,128)S(1)}, f32[3,1,768,128]{3,2,1,0:T(8,128)S(1)}, u32[]{:S(2)}, u32[]{:S(2)}) %collective-permute-start) | collective-permute-done | bytes 1179680 | tf_op jit(solution)/shard_map/ppermute | solution.py:252
  29.1 0.0 copy-done.4
  29.1 1.5 collective-permute-start.1
  30.6 6.4 %collective-permute-done.1 = f32[1,2,48,768]{3,2,1,0:T(8,128)S(1)} collective-permute-done((f32[1,2,48,768]{3,2,1,0:T(8,128)S(1)}, f32[1,2,48,768]{3,2,1,0:T(8,128)S(1)}, u32[]{:S(2)}, u32[]{:S(2)}) %collective-permute-start.1) | collective-permute-done | bytes 294944 | tf_op jit(solution)/shard_map/ppermute | solution.py:222
  37.1 0.5 collective-permute-start.2
  37.6 0.6 collective-permute-start.7
  38.2 12.2 %collective-permute-done.2 = f32[2,2,48,768]{3,2,1,0:T(8,128)S(1)} collective-permute-done((f32[2,2,48,768]{3,2,1,0:T(8,128)S(1)}, f32[2,2,48,768]{3,2,1,0:T(8,128)S(1)}, u32[]{:S(2)}, u32[]{:S(2)}) %collective-permute-start.2) | collective-permute-done | bytes 589856 | tf_op jit(solution)/shard_map/ppermute | solution.py:222
  50.4 0.1 broadcast_select_fusion.3
  50.5 1.1 pad_maximum_fusion.2
  51.7 2.6 %collective-permute-start.3 = (f32[4,2,48,768]{3,2,1,0:T(8,128)}, f32[4,2,48,768]{3,2,1,0:T(8,128)}, u32[]{:S(2)}, u32[]{:S(2)}) collective-permute-start(f32[4,2,48,768]{3,2,1,0:T(8,128)} %pad_maximum_fusion.2), channel_id=1, source_target_pairs={{0,16},{2,18},{4,20},{6,22},{8,24},{10,26},{12,28},{14,30},{16,0},... | collective-permute-start | bytes 3538952 | tf_op jit(solution)/shard_map/ppermute | solution.py:222
  54.3 17.3 %copy.9 = f32[3,14,768,128]{2,3,1,0:T(8,128)} copy(f32[3,14,768,128]{3,2,1,0:T(8,128)} %refs_0_) | data formatting | bytes 33030144 | tf_op jit(solution)/shard_map/optimization_barrier | solution.py:256
  71.6 0.0 copy-start.2
  71.6 0.0 copy-start.3
  71.6 1.4 slice_bitcast_fusion.1
  72.9 0.1 collective-permute-start.4
  73.0 2.6 %collective-permute-start.5 = (f32[3,8,3,768]{3,2,1,0:T(4,128)S(1)}, f32[3,8,3,768]{3,2,1,0:T(4,128)}, u32[]{:S(2)}, u32[]{:S(2)}) collective-permute-start(f32[3,8,3,768]{3,2,1,0:T(4,128)S(1)} %get-tuple-element.30), channel_id=1, source_target_pairs={{2,0},{4,2},{6,4},{8,6},{10,8},{12,10},{14,12},{16,14},{18,16},{20... | collective-permute-start | bytes 663560 | tf_op jit(solution)/shard_map/ppermute | solution.py:267
  75.6 0.1 pad.8.clone
  75.7 6.5 %collective-permute-done.4 = f32[3,8,3,768]{3,2,1,0:T(4,128)S(1)} collective-permute-done((f32[3,8,3,768]{3,2,1,0:T(4,128)S(1)}, f32[3,8,3,768]{3,2,1,0:T(4,128)S(1)}, u32[]{:S(2)}, u32[]{:S(2)}) %collective-permute-start.4) | collective-permute-done | bytes 221216 | tf_op jit(solution)/shard_map/ppermute | solution.py:266
  82.2 21.8 %collective-permute-done.5 = f32[3,8,3,768]{3,2,1,0:T(4,128)} collective-permute-done((f32[3,8,3,768]{3,2,1,0:T(4,128)S(1)}, f32[3,8,3,768]{3,2,1,0:T(4,128)}, u32[]{:S(2)}, u32[]{:S(2)}) %collective-permute-start.5) | collective-permute-done | bytes 221216 | tf_op jit(solution)/shard_map/ppermute | solution.py:267
  104.0 1.1 maximum_maximum_fusion.halo_ref
  105.1 0.0 copy-done.2
  105.1 0.0 copy-done.3
  105.2 0.0 copy-start
  105.2 5.7 %copy-done = f32[3,14,768,128]{3,2,1,0:T(8,128)S(1)} copy-done((f32[3,14,768,128]{3,2,1,0:T(8,128)S(1)}, f32[3,14,768,128]{3,2,1,0:T(8,128)}, u32[]{:S(2)}) %copy-start) | copy-done | bytes 16515096
  110.9 15.5 %stencils.1.acc_ref = f32[3,8,768,128]{3,2,1,0:T(8,128)} custom-call(f32[3,14,768,128]{3,2,1,0:T(8,128)S(1)} %copy-done, f32[3,8,8,768]{3,2,1,0:T(8,128)S(1)} %maximum_maximum_fusion.halo_ref, bf16[128,128]{1,0:T(8,128)(2,1)S(1)} %copy-done.2, f32[8,128]{1,0:T(8,128)S(1)} %copy-done.3), custom_call_target="tpu_custom_call" | custom-call | flops 1207959552 | bytes 25952256 | tf_op jit(solution)/shard_map/stencils/pallas_call | solution.py:68
  126.4 0.0 collective-permute-done.3
  126.4 1.5 broadcast_select_fusion.1
  127.8 0.2 pad_maximum_fusion.1
  128.1 0.1 collective-permute-start.6
  128.2 0.1 pad.5.clone
  128.3 0.1 add_add_fusion
  128.3 0.1 reshape.48.flags
  128.4 1.2 collective-permute-start.8
  129.7 3.1 %collective-permute-done.6 = f32[8,2,48,768]{3,2,1,0:T(8,128)} collective-permute-done((f32[8,2,48,768]{3,2,1,0:T(8,128)S(1)}, f32[8,2,48,768]{3,2,1,0:T(8,128)}, u32[]{:S(2)}, u32[]{:S(2)}) %collective-permute-start.6) | collective-permute-done | bytes 2359328 | tf_op jit(solution)/shard_map/ppermute | solution.py:222
  132.8 2.1 select_bitcast_fusion.1
  134.9 0.5 pad_maximum_fusion.piece_ref
  135.4 9.9 %weights.1 = (bf16[2,768,768]{2,1,0:T(8,128)(2,1)S(1)}, bf16[2,768,768]{2,1,0:T(8,128)(2,1)S(1)}) custom-call(s32[8]{0:T(128)S(1)} %reshape.48.flags, f32[2,8,2,48,768]{4,3,2,1,0:T(8,128)S(1)} %pad_maximum_fusion.piece_ref), custom_call_target="tpu_custom_call" | custom-call | flops 7247757312 | bytes 14155776 | tf_op jit(solution)/shard_map/weights/pallas_call | solution.py:137
  145.3 0.0 copy-start.1
  145.3 5.7 %copy-done.1 = f32[3,14,768,128]{3,2,1,0:T(8,128)S(1)} copy-done((f32[3,14,768,128]{3,2,1,0:T(8,128)S(1)}, f32[3,14,768,128]{3,2,1,0:T(8,128)}, u32[]{:S(2)}) %copy-start.1) | copy-done | bytes 16515096
  151.0 19.1 %column.4.acc_ref = f32[3,8,768,128]{3,2,1,0:T(8,128)} custom-call(f32[3,8,768,128]{3,2,1,0:T(8,128)} %stencils.1.acc_ref, bf16[2,768,768]{2,1,0:T(8,128)(2,1)S(1)} %get-tuple-element.24.high_ref, bf16[2,768,768]{2,1,0:T(8,128)(2,1)S(1)} %get-tuple-element.25.low_ref, f32[3,14,768,128]{3,2,1,0:T(8,128)S(1)} %copy-done.1), custom_call_target="tpu_custom_call", output_to_operand_aliasing={{}: (0, {})} | custom-call | flops 10871635968 | bytes 30670848 | tf_op jit(solution)/shard_map/column/pallas_call | solution.py:192
  170.2 4.3 %column.5.acc_ref = f32[3,8,768,128]{3,2,1,0:T(8,128)} custom-call(f32[3,8,768,128]{3,2,1,0:T(8,128)} %column.4.acc_ref, bf16[2,768,768]{2,1,0:T(8,128)(2,1)S(1)} %get-tuple-element.24.high_ref, bf16[2,768,768]{2,1,0:T(8,128)(2,1)S(1)} %get-tuple-element.25.low_ref, f32[3,1,768,128]{3,2,1,0:T(8,128)S(1)} %collective-permute-done.refs_0_), custom_call_target="tpu_custom_call", output_to_operand_aliasing={{}: (0, {})} | custom-call | flops 1358954496 | bytes 5898240 | tf_op jit(solution)/shard_map/column/pallas_call | solution.py:192
  174.5 18.8 %collective-permute-done.7.refs_0_ = f32[3,6,768,128]{3,2,1,0:T(8,128)} collective-permute-done((f32[3,6,768,128]{3,2,1,0:T(8,128)}, f32[3,6,768,128]{3,2,1,0:T(8,128)}, u32[]{:S(2)}, u32[]{:S(2)}) %collective-permute-start.7) | collective-permute-done | bytes 7077920 | tf_op jit(solution)/shard_map/ppermute | solution.py:252
  193.2 15.0 %column.6.acc_ref = f32[3,8,768,128]{3,2,1,0:T(8,128)} custom-call(f32[3,8,768,128]{3,2,1,0:T(8,128)} %column.5.acc_ref, bf16[2,768,768]{2,1,0:T(8,128)(2,1)S(1)} %get-tuple-element.24.high_ref, bf16[2,768,768]{2,1,0:T(8,128)(2,1)S(1)} %get-tuple-element.25.low_ref, f32[3,6,768,128]{3,2,1,0:T(8,128)} %collective-permute-done.7.refs_0_), custom_call_target="tpu_custom_call", output_to_operand_aliasing={{}: (0, {})} | custom-call | flops 8153726976 | bytes 23592960 | tf_op jit(solution)/shard_map/column/pallas_call | solution.py:192
  208.3 6.9 %collective-permute-done.8.refs_0_ = f32[3,1,768,128]{3,2,1,0:T(8,128)S(1)} collective-permute-done((f32[3,1,768,128]{3,2,1,0:T(8,128)}, f32[3,1,768,128]{3,2,1,0:T(8,128)S(1)}, u32[]{:S(2)}, u32[]{:S(2)}) %collective-permute-start.8) | collective-permute-done | bytes 1179680 | tf_op jit(solution)/shard_map/ppermute | solution.py:252
  215.1 4.3 %column.7 = f32[3,8,768,128]{3,2,1,0:T(8,128)} custom-call(f32[3,8,768,128]{3,2,1,0:T(8,128)} %column.6.acc_ref, bf16[2,768,768]{2,1,0:T(8,128)(2,1)S(1)} %get-tuple-element.24.high_ref, bf16[2,768,768]{2,1,0:T(8,128)(2,1)S(1)} %get-tuple-element.25.low_ref, f32[3,1,768,128]{3,2,1,0:T(8,128)S(1)} %collective-permute-done.8.refs_0_), custom_call_target="tpu_custom_call", output_to_operand_aliasing={{}: (0, {})} | custom-call | flops 1358954496 | bytes 5898240 | tf_op jit(solution)/shard_map/column/pallas_call | solution.py:192
  (5 shorter events, 0.1 us)
Async XLA Ops:
  1.4 27.8 %collective-permute-start = (f32[3,1,768,128]{3,2,1,0:T(8,128)S(1)}, f32[3,1,768,128]{3,2,1,0:T(8,128)S(1)}, u32[]{:S(2)}, u32[]{:S(2)}) collective-permute-start(f32[3,1,768,128]{3,2,1,0:T(8,128)S(1)} %slice.18), channel_id=1, source_target_pairs={{1,0},{0,1},{3,2},{2,3},{5,4},{4,5},{7,6},{6,7},{9,8},{8,9},{11,10... | collective-permute-start | bytes 3538952 | tf_op jit(solution)/shard_map/ppermute | solution.py:252
  8.4 20.7 %copy-start.4 = (f32[2,48,768]{2,1,0:T(8,128)S(1)}, f32[2,48,768]{2,1,0:T(8,128)}, u32[]{:S(2)}) copy-start(f32[2,48,768]{2,1,0:T(8,128)} %param.5) | copy-start | bytes 884740
  29.1 7.9 %collective-permute-start.1 = (f32[1,2,48,768]{3,2,1,0:T(8,128)S(1)}, f32[1,2,48,768]{3,2,1,0:T(8,128)S(1)}, u32[]{:S(2)}, u32[]{:S(2)}) collective-permute-start(f32[1,2,48,768]{3,2,1,0:T(8,128)S(1)} %bitcast.12), channel_id=1, source_target_pairs={{0,4},{2,6},{4,0},{6,2},{8,12},{10,14},{12,8},{14,10},{16,20},{18,... | collective-permute-start | bytes 884744 | tf_op jit(solution)/shard_map/ppermute | solution.py:222
  37.1 13.3 %collective-permute-start.2 = (f32[2,2,48,768]{3,2,1,0:T(8,128)S(1)}, f32[2,2,48,768]{3,2,1,0:T(8,128)S(1)}, u32[]{:S(2)}, u32[]{:S(2)}) collective-permute-start(f32[2,2,48,768]{3,2,1,0:T(8,128)S(1)} %pad_maximum_fusion.3), channel_id=1, source_target_pairs={{0,8},{2,10},{4,12},{6,14},{8,0},{10,2},{12,4},{14,6},{16,24},{18,... | collective-permute-start | bytes 1769480 | tf_op jit(solution)/shard_map/ppermute | solution.py:222
  37.6 155.6 %collective-permute-start.7 = (f32[3,6,768,128]{3,2,1,0:T(8,128)}, f32[3,6,768,128]{3,2,1,0:T(8,128)}, u32[]{:S(2)}, u32[]{:S(2)}) collective-permute-start(f32[3,6,768,128]{3,2,1,0:T(8,128)} %slice.19), channel_id=1, source_target_pairs={{1,0},{0,1},{3,2},{2,3},{5,4},{4,5},{7,6},{6,7},{9,8},{8,9},{11,10... | collective-permute-start | bytes 21233672 | tf_op jit(solution)/shard_map/ppermute | solution.py:252
  51.7 74.7 %collective-permute-start.3 = (f32[4,2,48,768]{3,2,1,0:T(8,128)}, f32[4,2,48,768]{3,2,1,0:T(8,128)}, u32[]{:S(2)}, u32[]{:S(2)}) collective-permute-start(f32[4,2,48,768]{3,2,1,0:T(8,128)} %pad_maximum_fusion.2), channel_id=1, source_target_pairs={{0,16},{2,18},{4,20},{6,22},{8,24},{10,26},{12,28},{14,30},{16,0},... | collective-permute-start | bytes 3538952 | tf_op jit(solution)/shard_map/ppermute | solution.py:222
  71.6 33.6 %copy-start.2 = (bf16[128,128]{1,0:T(8,128)(2,1)S(1)}, bf16[128,128]{1,0:T(8,128)(2,1)}, u32[]{:S(2)}) copy-start(bf16[128,128]{1,0:T(8,128)(2,1)} %constant.27.clone.inside_ref) | copy-start | bytes 98308
  71.6 33.6 %copy-start.3 = (f32[8,128]{1,0:T(8,128)S(1)}, f32[8,128]{1,0:T(8,128)}, u32[]{:S(2)}) copy-start(f32[8,128]{1,0:T(8,128)} %constant.28.clone.rim_ref) | copy-start | bytes 12292
  72.9 9.3 %collective-permute-start.4 = (f32[3,8,3,768]{3,2,1,0:T(4,128)S(1)}, f32[3,8,3,768]{3,2,1,0:T(4,128)S(1)}, u32[]{:S(2)}, u32[]{:S(2)}) collective-permute-start(f32[3,8,3,768]{3,2,1,0:T(4,128)S(1)} %get-tuple-element.29), channel_id=1, source_target_pairs={{30,0},{0,2},{2,4},{4,6},{6,8},{8,10},{10,12},{12,14},{14,16},{16,... | collective-permute-start | bytes 663560 | tf_op jit(solution)/shard_map/ppermute | solution.py:266
  73.0 31.0 %collective-permute-start.5 = (f32[3,8,3,768]{3,2,1,0:T(4,128)S(1)}, f32[3,8,3,768]{3,2,1,0:T(4,128)}, u32[]{:S(2)}, u32[]{:S(2)}) collective-permute-start(f32[3,8,3,768]{3,2,1,0:T(4,128)S(1)} %get-tuple-element.30), channel_id=1, source_target_pairs={{2,0},{4,2},{6,4},{8,6},{10,8},{12,10},{14,12},{16,14},{18,16},{20... | collective-permute-start | bytes 663560 | tf_op jit(solution)/shard_map/ppermute | solution.py:267
  105.2 5.7 %copy-start = (f32[3,14,768,128]{3,2,1,0:T(8,128)S(1)}, f32[3,14,768,128]{3,2,1,0:T(8,128)}, u32[]{:S(2)}) copy-start(f32[3,14,768,128]{3,2,1,0:T(8,128)} %refs_0_) | copy-start | bytes 49545220
  128.1 4.7 %collective-permute-start.6 = (f32[8,2,48,768]{3,2,1,0:T(8,128)S(1)}, f32[8,2,48,768]{3,2,1,0:T(8,128)}, u32[]{:S(2)}, u32[]{:S(2)}) collective-permute-start(f32[8,2,48,768]{3,2,1,0:T(8,128)S(1)} %pad_maximum_fusion.1), channel_id=1, source_target_pairs={{0,2},{2,0},{4,6},{6,4},{8,10},{10,8},{12,14},{14,12},{16,18},{18,... | collective-permute-start | bytes 7077896 | tf_op jit(solution)/shard_map/ppermute | solution.py:222
  128.4 86.7 %collective-permute-start.8 = (f32[3,1,768,128]{3,2,1,0:T(8,128)}, f32[3,1,768,128]{3,2,1,0:T(8,128)S(1)}, u32[]{:S(2)}, u32[]{:S(2)}) collective-permute-start(f32[3,1,768,128]{3,2,1,0:T(8,128)} %slice.20), channel_id=1, source_target_pairs={{1,0},{0,1},{3,2},{2,3},{5,4},{4,5},{7,6},{6,7},{9,8},{8,9},{11,10... | collective-permute-start | bytes 3538952 | tf_op jit(solution)/shard_map/ppermute | solution.py:252
  145.3 5.7 %copy-start.1 = (f32[3,14,768,128]{3,2,1,0:T(8,128)S(1)}, f32[3,14,768,128]{3,2,1,0:T(8,128)}, u32[]{:S(2)}) copy-start(f32[3,14,768,128]{3,2,1,0:T(8,128)} %refs_0_) | copy-start | bytes 49545220

commit v3 on v2

--- a/solution.py
+++ b/solution.py
@@ -11,6 +11,7 @@
 RIM = 3
 WEIGHTS = ((1, 45.0), (2, -9.0), (3, 1.0))
 CHUNKS = (1, 6, 1)
+BRIEF = pl.CostEstimate(flops=1000, bytes_accessed=1000, transcendentals=0)
 
 
 def stencil_matrices(width):
@@ -77,11 +78,7 @@
         out_specs=pl.BlockSpec((3, planes, tile, width), lambda t: (0, 0, t, 0)),
         out_shape=jax.ShapeDtypeStruct((3, planes, rows, width), jnp.float32),
         compiler_params=pltpu.CompilerParams(vmem_limit_bytes=24 << 20),
-        cost_estimate=pl.CostEstimate(
-            flops=12 * planes * rows * width * width,
-            bytes_accessed=4 * 3 * (held + planes) * rows * width,
-            transcendentals=0,
-        ),
+        cost_estimate=BRIEF,
         name="stencils",
     )(velocity, halo, jnp.asarray(inside, jnp.bfloat16), jnp.asarray(rim))
 
@@ -151,11 +148,7 @@
         ),
         out_shape=[shape, shape],
         compiler_params=pltpu.CompilerParams(vmem_limit_bytes=24 << 20),
-        cost_estimate=pl.CostEstimate(
-            flops=8 * count * rows * rows * rows,
-            bytes_accessed=count * rows * (8 * halfway + 4 * rows),
-            transcendentals=0,
-        ),
+        cost_estimate=BRIEF,
         name="weights",
     )(flags, piece)
 
@@ -198,11 +191,7 @@
         out_shape=jax.ShapeDtypeStruct(acc.shape, acc.dtype),
         input_output_aliases={0: 0},
         compiler_params=pltpu.CompilerParams(vmem_limit_bytes=32 << 20),
-        cost_estimate=pl.CostEstimate(
-            flops=18 * planes * count * rows * rows * width,
-            bytes_accessed=4 * 3 * planes * (2 + count) * rows * width + 4 * count * rows * rows,
-            transcendentals=0,
-        ),
+        cost_estimate=BRIEF,
         name="column",
     )(acc, high, low, *lines)
 

time: 223 us -> 213 us (0.955)
  waiting for transfers between devices: 94 us -> 80.6 us
  other arithmetic: 6.76 us -> 9.98 us
    ppermute x3, waiting for transfers between devices: 43.9 us -> 32.8 us  [send(): return [lax.ppermute(part, 'gy', around(count, s)) for s in range(1, count)]]
    unnamed x10 -> x12, local copies, waits for them, and re-layouts: 11.4 us -> 11.4 us
  transfers between devices with their start and end apart: 9 -> 9, of which waited for: 8 -> 8; matrix products, arithmetic and copies ran while one was open for 16% -> 18% of each run, Pallas kernels for 29% -> 30%
where the time goes in v3:
time: 213 us; the launch traced here: 210 us
  waiting for transfers between devices  80.6 us (38%)
  Pallas kernels  68.2 us (32%)
  local copies, waits for them, and re-layouts  40.5 us (19%)
  starting transfers between devices  10.9 us (5%)
  other arithmetic  9.98 us (5%)
    pallas_call x4, Pallas kernels, add_column(): pl.pallas_call(functools.partial(column_kernel, first_in_block, count), g...  42.8 us
    ppermute x3, waiting for transfers between devices, send(): return [lax.ppermute(part, 'gy', around(count, s)) for s in range(1, count)]  32.8 us
    ppermute x1, waiting for transfers between devices, shards(): right = lax.ppermute(right, 'gx', around(ring, 1))  22.1 us
    ppermute x4, waiting for transfers between devices, exchange(): other = lax.ppermute(held, 'gx', [(i, i ^ 1 << bit) for i in range(ring)])  20.3 us
    optimization_barrier x1, local copies, waits for them, and re-layouts, shards(): lax.optimization_barrier((velocity, plane_range(velocity, *cuts[1])))  17.3 us
    pallas_call x1, Pallas kernels, stencils(): pl.pallas_call(stencil_kernel, grid=(rows // tile,), in_specs=[pl.BlockSp...  15.5 us
    unnamed x12, local copies, waits for them, and re-layouts  11.4 us
    slice x3, local copies, waits for them, and re-layouts, plane_range(): return lax.slice_in_dim(field, RIM + start, RIM + start + size, axis=1)  10.2 us
  transfers between devices with their start and end apart: 9, of which 8 were waited for; matrix products, arithmetic and copies ran while one was open for 18% of the time, Pallas kernels for 30%

profile of v3, /device:TPU:12, one launch (start us, length us, event | category | flops | bytes accessed | tf_op | source)
XLA Modules:
  0.0 210.4 jit_solution(760052950082336984)
XLA Ops:
  0.0 1.3 slice.18
  1.4 0.6 collective-permute-start
  1.9 6.5 %slice.19 = f32[3,6,768,128]{3,2,1,0:T(8,128)} slice(f32[3,14,768,128]{3,2,1,0:T(8,128)} %refs_0_), slice={[0:3], [4:10], [0:768], [0:128]} | slice | bytes 14155776 | tf_op jit(solution)/shard_map/slice | solution.py:238
  8.5 0.0 copy-start.5
  8.5 1.5 collective-permute-start.7
  10.0 2.4 %slice.20 = f32[3,1,768,128]{3,2,1,0:T(8,128)} slice(f32[3,14,768,128]{3,2,1,0:T(8,128)} %refs_0_), slice={[0:3], [10:11], [0:768], [0:128]} | slice | bytes 2359296 | tf_op jit(solution)/shard_map/slice | solution.py:238
  12.3 17.9 %collective-permute-done.refs_0_ = f32[3,1,768,128]{3,2,1,0:T(8,128)S(1)} collective-permute-done((f32[3,1,768,128]{3,2,1,0:T(8,128)S(1)}, f32[3,1,768,128]{3,2,1,0:T(8,128)S(1)}, u32[]{:S(2)}, u32[]{:S(2)}) %collective-permute-start) | collective-permute-done | bytes 1179680 | tf_op jit(solution)/shard_map/ppermute | solution.py:241
  30.3 0.0 copy-done.5
  30.3 1.5 collective-permute-start.1
  31.8 5.2 %collective-permute-done.1 = f32[1,2,48,768]{3,2,1,0:T(8,128)S(1)} collective-permute-done((f32[1,2,48,768]{3,2,1,0:T(8,128)S(1)}, f32[1,2,48,768]{3,2,1,0:T(8,128)S(1)}, u32[]{:S(2)}, u32[]{:S(2)}) %collective-permute-start.1) | collective-permute-done | bytes 294944 | tf_op jit(solution)/shard_map/ppermute | solution.py:211
  37.1 0.5 collective-permute-start.2
  37.6 11.9 %collective-permute-done.2 = f32[2,2,48,768]{3,2,1,0:T(8,128)} collective-permute-done((f32[2,2,48,768]{3,2,1,0:T(8,128)S(1)}, f32[2,2,48,768]{3,2,1,0:T(8,128)}, u32[]{:S(2)}, u32[]{:S(2)}) %collective-permute-start.2) | collective-permute-done | bytes 589856 | tf_op jit(solution)/shard_map/ppermute | solution.py:211
  49.6 1.2 broadcast_select_fusion.3
  50.7 1.1 pad_maximum_fusion.2
  51.8 2.6 %collective-permute-start.3 = (f32[4,2,48,768]{3,2,1,0:T(8,128)}, f32[4,2,48,768]{3,2,1,0:T(8,128)}, u32[]{:S(2)}, u32[]{:S(2)}) collective-permute-start(f32[4,2,48,768]{3,2,1,0:T(8,128)} %pad_maximum_fusion.2), channel_id=1, source_target_pairs={{0,16},{2,18},{4,20},{6,22},{8,24},{10,26},{12,28},{14,30},{16,0},... | collective-permute-start | bytes 3538952 | tf_op jit(solution)/shard_map/ppermute | solution.py:211
  54.4 17.3 %copy.9 = f32[3,14,768,128]{2,3,1,0:T(8,128)} copy(f32[3,14,768,128]{3,2,1,0:T(8,128)} %refs_0_) | data formatting | bytes 33030144 | tf_op jit(solution)/shard_map/optimization_barrier | solution.py:245
  71.7 0.0 copy-start.2
  71.7 0.0 copy-start.3
  71.7 1.4 slice_bitcast_fusion.1
  73.1 0.1 collective-permute-start.4
  73.1 2.6 %collective-permute-start.5 = (f32[3,8,3,768]{3,2,1,0:T(4,128)S(1)}, f32[3,8,3,768]{3,2,1,0:T(4,128)}, u32[]{:S(2)}, u32[]{:S(2)}) collective-permute-start(f32[3,8,3,768]{3,2,1,0:T(4,128)S(1)} %get-tuple-element.30), channel_id=1, source_target_pairs={{2,0},{4,2},{6,4},{8,6},{10,8},{12,10},{14,12},{16,14},{18,16},{20... | collective-permute-start | bytes 663560 | tf_op jit(solution)/shard_map/ppermute | solution.py:256
  75.8 0.1 pad.8.clone
  75.8 5.5 %collective-permute-done.4 = f32[3,8,3,768]{3,2,1,0:T(4,128)S(1)} collective-permute-done((f32[3,8,3,768]{3,2,1,0:T(4,128)S(1)}, f32[3,8,3,768]{3,2,1,0:T(4,128)S(1)}, u32[]{:S(2)}, u32[]{:S(2)}) %collective-permute-start.4) | collective-permute-done | bytes 221216 | tf_op jit(solution)/shard_map/ppermute | solution.py:255
  81.3 22.1 %collective-permute-done.5 = f32[3,8,3,768]{3,2,1,0:T(4,128)} collective-permute-done((f32[3,8,3,768]{3,2,1,0:T(4,128)S(1)}, f32[3,8,3,768]{3,2,1,0:T(4,128)}, u32[]{:S(2)}, u32[]{:S(2)}) %collective-permute-start.5) | collective-permute-done | bytes 221216 | tf_op jit(solution)/shard_map/ppermute | solution.py:256
  103.4 1.1 maximum_maximum_fusion.halo_ref
  104.5 0.0 copy-done.2
  104.5 0.0 copy-done.3
  104.5 0.0 copy-start
  104.5 5.7 %copy-done = f32[3,14,768,128]{3,2,1,0:T(8,128)S(1)} copy-done((f32[3,14,768,128]{3,2,1,0:T(8,128)S(1)}, f32[3,14,768,128]{3,2,1,0:T(8,128)}, u32[]{:S(2)}) %copy-start) | copy-done | bytes 16515096
  110.2 15.5 %stencils.1.acc_ref = f32[3,8,768,128]{3,2,1,0:T(8,128)} custom-call(f32[3,14,768,128]{3,2,1,0:T(8,128)S(1)} %copy-done, f32[3,8,8,768]{3,2,1,0:T(8,128)S(1)} %maximum_maximum_fusion.halo_ref, bf16[128,128]{1,0:T(8,128)(2,1)S(1)} %copy-done.2, f32[8,128]{1,0:T(8,128)S(1)} %copy-done.3), custom_call_target="tpu_custom_call" | custom-call | flops 1000 | bytes 1000 | tf_op jit(solution)/shard_map/stencils/pallas_call | solution.py:69
  125.7 0.0 collective-permute-done.3
  125.7 1.5 broadcast_select_fusion.1
  127.2 0.0 copy-start.4
  127.2 1.7 pad_maximum_fusion.1
  128.8 0.0 collective-permute-start.6
  128.8 0.0 copy-done.4
  128.9 1.5 collective-permute-start.8
  130.4 0.1 pad.5.clone
  130.5 0.1 add_add_fusion
  130.5 0.1 reshape.48.flags
  130.6 3.1 %collective-permute-done.6 = f32[8,2,48,768]{3,2,1,0:T(8,128)} collective-permute-done((f32[8,2,48,768]{3,2,1,0:T(8,128)}, f32[8,2,48,768]{3,2,1,0:T(8,128)}, u32[]{:S(2)}, u32[]{:S(2)}) %collective-permute-start.6) | collective-permute-done | bytes 2359328 | tf_op jit(solution)/shard_map/ppermute | solution.py:211
  133.7 2.8 %select_bitcast_fusion.1 = (f32[1,8,2,48,768]{4,3,2,1,0:T(8,128)S(1)}, f32[1,8,2,48,768]{4,3,2,1,0:T(8,128)S(1)}) fusion(f32[8,2,48,768]{3,2,1,0:T(8,128)} %collective-permute-done.6, f32[8,2,48,768]{3,2,1,0:T(8,128)} %pad_maximum_fusion.1, pred[]{:T(512)S(6)} %eq.30), kind=kLoop, calls=%fused_computation.3 | loop fusion | flops 1179648 | bytes 9437185 | tf_op jit(solution)/shard_map/stack | solution.py:213
  136.6 0.5 pad_maximum_fusion.piece_ref
  137.0 9.9 %weights.1 = (bf16[2,768,768]{2,1,0:T(8,128)(2,1)S(1)}, bf16[2,768,768]{2,1,0:T(8,128)(2,1)S(1)}) custom-call(s32[8]{0:T(128)S(1)} %reshape.48.flags, f32[2,8,2,48,768]{4,3,2,1,0:T(8,128)S(1)} %pad_maximum_fusion.piece_ref), custom_call_target="tpu_custom_call" | custom-call | flops 1000 | bytes 1000 | tf_op jit(solution)/shard_map/weights/pallas_call | solution.py:134
  147.0 0.0 copy-start.1
  147.0 5.7 %copy-done.1 = f32[3,14,768,128]{3,2,1,0:T(8,128)S(1)} copy-done((f32[3,14,768,128]{3,2,1,0:T(8,128)S(1)}, f32[3,14,768,128]{3,2,1,0:T(8,128)}, u32[]{:S(2)}) %copy-start.1) | copy-done | bytes 16515096
  152.7 19.1 %column.4.acc_ref = f32[3,8,768,128]{3,2,1,0:T(8,128)} custom-call(f32[3,8,768,128]{3,2,1,0:T(8,128)} %stencils.1.acc_ref, bf16[2,768,768]{2,1,0:T(8,128)(2,1)S(1)} %get-tuple-element.24.high_ref, bf16[2,768,768]{2,1,0:T(8,128)(2,1)S(1)} %get-tuple-element.25.low_ref, f32[3,14,768,128]{3,2,1,0:T(8,128)S(1)} %copy-done.1), custom_call_target="tpu_custom_call", output_to_operand_aliasing={{}: (0, {})} | custom-call | flops 1000 | bytes 1000 | tf_op jit(solution)/shard_map/column/pallas_call | solution.py:185
  171.8 4.3 %column.5.acc_ref = f32[3,8,768,128]{3,2,1,0:T(8,128)} custom-call(f32[3,8,768,128]{3,2,1,0:T(8,128)} %column.4.acc_ref, bf16[2,768,768]{2,1,0:T(8,128)(2,1)S(1)} %get-tuple-element.24.high_ref, bf16[2,768,768]{2,1,0:T(8,128)(2,1)S(1)} %get-tuple-element.25.low_ref, f32[3,1,768,128]{3,2,1,0:T(8,128)S(1)} %collective-permute-done.refs_0_), custom_call_target="tpu_custom_call", output_to_operand_aliasing={{}: (0, {})} | custom-call | flops 1000 | bytes 1000 | tf_op jit(solution)/shard_map/column/pallas_call | solution.py:185
  176.1 5.9 %collective-permute-done.7.refs_0_ = f32[3,6,768,128]{3,2,1,0:T(8,128)} collective-permute-done((f32[3,6,768,128]{3,2,1,0:T(8,128)}, f32[3,6,768,128]{3,2,1,0:T(8,128)}, u32[]{:S(2)}, u32[]{:S(2)}) %collective-permute-start.7) | collective-permute-done | bytes 7077920 | tf_op jit(solution)/shard_map/ppermute | solution.py:241
  182.1 15.0 %column.6.acc_ref = f32[3,8,768,128]{3,2,1,0:T(8,128)} custom-call(f32[3,8,768,128]{3,2,1,0:T(8,128)} %column.5.acc_ref, bf16[2,768,768]{2,1,0:T(8,128)(2,1)S(1)} %get-tuple-element.24.high_ref, bf16[2,768,768]{2,1,0:T(8,128)(2,1)S(1)} %get-tuple-element.25.low_ref, f32[3,6,768,128]{3,2,1,0:T(8,128)} %collective-permute-done.7.refs_0_), custom_call_target="tpu_custom_call", output_to_operand_aliasing={{}: (0, {})} | custom-call | flops 1000 | bytes 1000 | tf_op jit(solution)/shard_map/column/pallas_call | solution.py:185
  197.1 9.0 %collective-permute-done.8.refs_0_ = f32[3,1,768,128]{3,2,1,0:T(8,128)S(1)} collective-permute-done((f32[3,1,768,128]{3,2,1,0:T(8,128)S(1)}, f32[3,1,768,128]{3,2,1,0:T(8,128)S(1)}, u32[]{:S(2)}, u32[]{:S(2)}) %collective-permute-start.8) | collective-permute-done | bytes 1179680 | tf_op jit(solution)/shard_map/ppermute | solution.py:241
  206.1 4.3 %column.7 = f32[3,8,768,128]{3,2,1,0:T(8,128)} custom-call(f32[3,8,768,128]{3,2,1,0:T(8,128)} %column.6.acc_ref, bf16[2,768,768]{2,1,0:T(8,128)(2,1)S(1)} %get-tuple-element.24.high_ref, bf16[2,768,768]{2,1,0:T(8,128)(2,1)S(1)} %get-tuple-element.25.low_ref, f32[3,1,768,128]{3,2,1,0:T(8,128)S(1)} %collective-permute-done.8.refs_0_), custom_call_target="tpu_custom_call", output_to_operand_aliasing={{}: (0, {})} | custom-call | flops 1000 | bytes 1000 | tf_op jit(solution)/shard_map/column/pallas_call | solution.py:185
  (5 shorter events, 0.1 us)
Async XLA Ops:
  1.4 28.9 %collective-permute-start = (f32[3,1,768,128]{3,2,1,0:T(8,128)S(1)}, f32[3,1,768,128]{3,2,1,0:T(8,128)S(1)}, u32[]{:S(2)}, u32[]{:S(2)}) collective-permute-start(f32[3,1,768,128]{3,2,1,0:T(8,128)S(1)} %slice.18), channel_id=1, source_target_pairs={{1,0},{0,1},{3,2},{2,3},{5,4},{4,5},{7,6},{6,7},{9,8},{8,9},{11,10... | collective-permute-start | bytes 3538952 | tf_op jit(solution)/shard_map/ppermute | solution.py:241
  8.5 21.8 %copy-start.5 = (f32[2,48,768]{2,1,0:T(8,128)S(1)}, f32[2,48,768]{2,1,0:T(8,128)}, u32[]{:S(2)}) copy-start(f32[2,48,768]{2,1,0:T(8,128)} %param.5) | copy-start | bytes 884740
  8.5 173.6 %collective-permute-start.7 = (f32[3,6,768,128]{3,2,1,0:T(8,128)}, f32[3,6,768,128]{3,2,1,0:T(8,128)}, u32[]{:S(2)}, u32[]{:S(2)}) collective-permute-start(f32[3,6,768,128]{3,2,1,0:T(8,128)} %slice.19), channel_id=1, source_target_pairs={{1,0},{0,1},{3,2},{2,3},{5,4},{4,5},{7,6},{6,7},{9,8},{8,9},{11,10... | collective-permute-start | bytes 21233672 | tf_op jit(solution)/shard_map/ppermute | solution.py:241
  30.3 6.7 %collective-permute-start.1 = (f32[1,2,48,768]{3,2,1,0:T(8,128)S(1)}, f32[1,2,48,768]{3,2,1,0:T(8,128)S(1)}, u32[]{:S(2)}, u32[]{:S(2)}) collective-permute-start(f32[1,2,48,768]{3,2,1,0:T(8,128)S(1)} %bitcast.12), channel_id=1, source_target_pairs={{0,4},{2,6},{4,0},{6,2},{8,12},{10,14},{12,8},{14,10},{16,20},{18,... | collective-permute-start | bytes 884744 | tf_op jit(solution)/shard_map/ppermute | solution.py:211
  37.1 12.5 %collective-permute-start.2 = (f32[2,2,48,768]{3,2,1,0:T(8,128)S(1)}, f32[2,2,48,768]{3,2,1,0:T(8,128)}, u32[]{:S(2)}, u32[]{:S(2)}) collective-permute-start(f32[2,2,48,768]{3,2,1,0:T(8,128)S(1)} %pad_maximum_fusion.3), channel_id=1, source_target_pairs={{0,8},{2,10},{4,12},{6,14},{8,0},{10,2},{12,4},{14,6},{16,24},{18,... | collective-permute-start | bytes 1769480 | tf_op jit(solution)/shard_map/ppermute | solution.py:211
  51.8 73.9 %collective-permute-start.3 = (f32[4,2,48,768]{3,2,1,0:T(8,128)}, f32[4,2,48,768]{3,2,1,0:T(8,128)}, u32[]{:S(2)}, u32[]{:S(2)}) collective-permute-start(f32[4,2,48,768]{3,2,1,0:T(8,128)} %pad_maximum_fusion.2), channel_id=1, source_target_pairs={{0,16},{2,18},{4,20},{6,22},{8,24},{10,26},{12,28},{14,30},{16,0},... | collective-permute-start | bytes 3538952 | tf_op jit(solution)/shard_map/ppermute | solution.py:211
  71.7 32.8 %copy-start.2 = (bf16[128,128]{1,0:T(8,128)(2,1)S(1)}, bf16[128,128]{1,0:T(8,128)(2,1)}, u32[]{:S(2)}) copy-start(bf16[128,128]{1,0:T(8,128)(2,1)} %constant.27.clone.inside_ref) | copy-start | bytes 98308
  71.7 32.8 %copy-start.3 = (f32[8,128]{1,0:T(8,128)S(1)}, f32[8,128]{1,0:T(8,128)}, u32[]{:S(2)}) copy-start(f32[8,128]{1,0:T(8,128)} %constant.28.clone.rim_ref) | copy-start | bytes 12292
  73.1 8.2 %collective-permute-start.4 = (f32[3,8,3,768]{3,2,1,0:T(4,128)S(1)}, f32[3,8,3,768]{3,2,1,0:T(4,128)S(1)}, u32[]{:S(2)}, u32[]{:S(2)}) collective-permute-start(f32[3,8,3,768]{3,2,1,0:T(4,128)S(1)} %get-tuple-element.29), channel_id=1, source_target_pairs={{30,0},{0,2},{2,4},{4,6},{6,8},{8,10},{10,12},{12,14},{14,16},{16,... | collective-permute-start | bytes 663560 | tf_op jit(solution)/shard_map/ppermute | solution.py:255
  73.1 30.2 %collective-permute-start.5 = (f32[3,8,3,768]{3,2,1,0:T(4,128)S(1)}, f32[3,8,3,768]{3,2,1,0:T(4,128)}, u32[]{:S(2)}, u32[]{:S(2)}) collective-permute-start(f32[3,8,3,768]{3,2,1,0:T(4,128)S(1)} %get-tuple-element.30), channel_id=1, source_target_pairs={{2,0},{4,2},{6,4},{8,6},{10,8},{12,10},{14,12},{16,14},{18,16},{20... | collective-permute-start | bytes 663560 | tf_op jit(solution)/shard_map/ppermute | solution.py:256
  104.5 5.7 %copy-start = (f32[3,14,768,128]{3,2,1,0:T(8,128)S(1)}, f32[3,14,768,128]{3,2,1,0:T(8,128)}, u32[]{:S(2)}) copy-start(f32[3,14,768,128]{3,2,1,0:T(8,128)} %refs_0_) | copy-start | bytes 49545220
  127.2 1.7 copy-start.4
  128.8 4.9 %collective-permute-start.6 = (f32[8,2,48,768]{3,2,1,0:T(8,128)}, f32[8,2,48,768]{3,2,1,0:T(8,128)}, u32[]{:S(2)}, u32[]{:S(2)}) collective-permute-start(f32[8,2,48,768]{3,2,1,0:T(8,128)} %pad_maximum_fusion.1), channel_id=1, source_target_pairs={{0,2},{2,0},{4,6},{6,4},{8,10},{10,8},{12,14},{14,12},{16,18},{18,... | collective-permute-start | bytes 7077896 | tf_op jit(solution)/shard_map/ppermute | solution.py:211
  128.9 77.2 %collective-permute-start.8 = (f32[3,1,768,128]{3,2,1,0:T(8,128)S(1)}, f32[3,1,768,128]{3,2,1,0:T(8,128)S(1)}, u32[]{:S(2)}, u32[]{:S(2)}) collective-permute-start(f32[3,1,768,128]{3,2,1,0:T(8,128)S(1)} %copy-done.4), channel_id=1, source_target_pairs={{1,0},{0,1},{3,2},{2,3},{5,4},{4,5},{7,6},{6,7},{9,8},{8,9},{11,10... | collective-permute-start | bytes 3538952 | tf_op jit(solution)/shard_map/ppermute | solution.py:241
  147.0 5.7 %copy-start.1 = (f32[3,14,768,128]{3,2,1,0:T(8,128)S(1)}, f32[3,14,768,128]{3,2,1,0:T(8,128)}, u32[]{:S(2)}) copy-start(f32[3,14,768,128]{3,2,1,0:T(8,128)} %refs_0_) | copy-start | bytes 49545220
